TPU v7x, 256 devices: a whole 4x4x8 slice. The times are simulated.
256 devices in a mesh: tgt: 32 (over z, y_hi, core), src: 8 (over y_lo, x).
Axes of the slice: x: 4, y: 4 (y_hi: 2, y_lo: 2; y = y_hi * 2 + y_lo), z: 8, core: 2. Of those that a mesh axis runs over, the one named last changes fastest.
Arguments:
- tgt_points: bfloat16 [3, 16384], P(None, 'tgt'), may hold values from -4 to 4
- tgt_weight: float32 [16384], P('tgt'), may hold values from 0.5 to 2
- src_points: bfloat16 [4, 3, 32768], P(None, None, ('tgt', 'src')), may hold values from -4 to 4
- src_weight: float32 [4, 32768], P(None, ('tgt', 'src')), may hold values from 0.5 to 2
- basis: float32 [4, 3, 32768], P(None, None, ('tgt', 'src')), may hold values from 0.05 to 1
- span: int32 [4, 32768], P(None, ('tgt', 'src')), may hold values from 0 to 29
- patch: int32 [4, 32768], P(None, ('tgt', 'src')), may hold values from 0 to 3
- patch_factor: float32 [4, 2, 1024], P(None, None, ('tgt', 'src')), may hold values from -1.5 to 1.5
- ctrl_weight: float32 [4, 8192], P(None, ('tgt', 'src')), may hold values from 0.5 to 2
- ctrl_coef: bfloat16 [4, 128, 8192], P(None, None, ('tgt', 'src')), may hold values from -6 to 6
- band: float32 [8, 16384], P(None, 'tgt'), may hold values from -0.5 to 0.5
- offsets: int32 [8], replicated, may hold values from -8 to 8, as said below
Outputs:
- shell_field: float32 [16384, 128], P('tgt')
Inputs may be any that keep to these rules, and one draw needn't show every extreme that they name: span of source point j is local to the 32 control points of the block j // 128. patch of source point j is local to the 4 patches of the block j // 128. offsets[0] is 8 and offsets[1] is -8.
All inputs are finite; a program needn't handle non-finite values.
Results may differ from a plain program's by a relative error of at most 0.0041.
Values may be sent and summed in bfloat16 or wider, within the bound.
No kernel may reach another device: no remote copies, remote signals or barrier semaphores. Data moves between devices by JAX's collectives and lax.ppermute only.
A program may use at most 128 MiB of HBM per device.

v0:
```python
import math

import jax
import jax.numpy as jnp
from jax import lax
from jax.sharding import PartitionSpec as P

HALO = 8


WAVE = 8.0
SMOOTH = 0.0025


def extended(block, sides, width):
    for axis, dim in sides:
        count = lax.axis_size(axis)
        forward = [(i, i + 1) for i in range(count - 1)]
        backward = [(target, source) for source, target in forward]
        low = lax.ppermute(
            lax.slice_in_dim(block, block.shape[dim] - width, None, axis=dim), axis, forward
        )
        high = lax.ppermute(lax.slice_in_dim(block, 0, width, axis=dim), axis, backward)
        block = jnp.concatenate([low, block, high], axis=dim)
    return block


def kernel_terms(targets, sources, density):
    tpos = targets.astype(jnp.float32)
    spos = sources.astype(jnp.float32)
    dist_sq = SMOOTH + (tpos[0][:, None] - spos[0][None, :]) ** 2
    dist_sq = dist_sq + (tpos[1][:, None] - spos[1][None, :]) ** 2
    dist_sq = dist_sq + (tpos[2][:, None] - spos[2][None, :]) ** 2
    dist = jnp.sqrt(dist_sq)
    kernel_re = (jnp.cos(WAVE * dist) / dist).astype(jnp.bfloat16)
    kernel_im = (jnp.sin(WAVE * dist) / dist).astype(jnp.bfloat16)
    dims = (((1,), (1,)), ((), ()))
    part_a = lax.dot_general(kernel_re, density, dims, preferred_element_type=jnp.float32)
    part_b = lax.dot_general(kernel_im, density, dims, preferred_element_type=jnp.float32)
    half = density.shape[0] // 2
    return jnp.concatenate(
        [part_a[:, :half] - part_b[:, half:], part_a[:, half:] + part_b[:, :half]], axis=1
    )


def block_density(weight, basis_rows, span_row, patch_row, factor_rows, weights_ctrl, coef_ctrl):
    count = weight.shape[0]
    fields = coef_ctrl.shape[0] // 2
    denom = jnp.zeros((count,), jnp.float32)
    numer = jnp.zeros((coef_ctrl.shape[0], count), jnp.float32)
    for basis_index in range(basis_rows.shape[0]):
        control_index = span_row + basis_index
        scaled = basis_rows[basis_index] * weights_ctrl[control_index]
        denom = denom + scaled
        numer = numer + scaled[None, :] * coef_ctrl[:, control_index].astype(jnp.float32)
    ratio = numer / denom[None, :]
    labels = jnp.arange(factor_rows.shape[1], dtype=jnp.int32)
    member = patch_row[None, :] == labels[:, None]
    factor_re = jnp.sum(jnp.where(member, factor_rows[0][:, None], 0.0), axis=0)
    factor_im = jnp.sum(jnp.where(member, factor_rows[1][:, None], 0.0), axis=0)
    ratio_re = ratio[:fields]
    ratio_im = ratio[fields:]
    dens_re = weight * (factor_re * ratio_re - factor_im * ratio_im)
    dens_im = weight * (factor_re * ratio_im + factor_im * ratio_re)
    return jnp.concatenate([dens_re, dens_im], axis=0).astype(jnp.bfloat16)


def add_kernel(carried, targets, geometry, density):
    width = geometry.shape[1]
    block_size = 1024

    def step_fn(index, inner):
        begin = index * block_size
        part_geo = lax.dynamic_slice_in_dim(geometry, begin, block_size, 1)
        part_den = lax.dynamic_slice_in_dim(density, begin, block_size, 1)
        return inner + kernel_terms(targets, part_geo, part_den)

    return lax.fori_loop(0, width // block_size, step_fn, carried)


def per_device(
    tgt_points,
    tgt_weight,
    src_points,
    src_weight,
    basis,
    span,
    patch,
    patch_factor,
    ctrl_weight,
    ctrl_coef,
    band,
    offsets,
):
    rows = tgt_points.shape[1]
    columns = ctrl_coef.shape[1]
    rounds = src_weight.shape[0]
    partial_value = jnp.zeros((rows, columns), jnp.float32)
    for section in range(rounds):
        density = block_density(
            src_weight[section],
            basis[section],
            span[section],
            patch[section],
            patch_factor[section],
            ctrl_weight[section],
            ctrl_coef[section],
        )
        geometry, gathered = (
            lax.all_gather(src_points[section], "tgt", axis=1, tiled=True),
            lax.all_gather(density, "tgt", axis=1, tiled=True),
        )
        partial_value = add_kernel(partial_value, tgt_points, geometry, gathered)
    total = lax.psum(partial_value, "src")
    source_count = rounds * src_weight.shape[1] * lax.axis_size("tgt") * lax.axis_size("src")
    scale = jnp.float32(1.0 / math.sqrt(source_count))
    potential = total * scale * tgt_weight[:, None]
    padded = extended(potential, (("tgt", 0),), HALO)
    shell_field = potential
    for diag in range(band.shape[0]):
        begin = HALO + offsets[diag]
        shifted = lax.dynamic_slice_in_dim(padded, begin, rows, 0)
        shell_field = shell_field + band[diag][:, None] * shifted
    return shell_field


def solution(mesh):
    in_specs = (
        P(None, "tgt"),
        P("tgt"),
        P(None, None, ("tgt", "src")),
        P(None, ("tgt", "src")),
        P(None, None, ("tgt", "src")),
        P(None, ("tgt", "src")),
        P(None, ("tgt", "src")),
        P(None, None, ("tgt", "src")),
        P(None, ("tgt", "src")),
        P(None, None, ("tgt", "src")),
        P(None, "tgt"),
        P(),
    )
    out_specs = P("tgt", None)
    return jax.shard_map(
        per_device, mesh=mesh, in_specs=in_specs, out_specs=out_specs, check_vma=False
    )
```

profile of v0, /device:TPU:1, one launch (start us, length us, event | category | flops | bytes accessed | tf_op | source)
XLA Modules:
  0.0 627.6 jit_solution(9285904822959095373)
XLA Ops:
  37.3 46.2 %all-gather = bf16[1,3,4096]{2,1,0:T(4,128)(2,1)S(1)} all-gather(bf16[1,3,128]{2,1,0:T(4,128)(2,1)S(1)} %copy.57), channel_id=2, replica_groups=mesh['tgt'=32,'src'=8] {'tgt'}, dimensions={2}, use_global_device_ids=true | all-gather | bytes 25344 | tf_op jit(solution)/shard_map/all_gather | solution.py:110
  83.5 36.7 %all-gather.1 = bf16[1,3,4096]{2,1,0:T(4,128)(2,1)S(1)} all-gather(bf16[1,3,128]{2,1,0:T(4,128)(2,1)S(1)} %copy.58), channel_id=3, replica_groups=mesh['tgt'=32,'src'=8] {'tgt'}, dimensions={2}, use_global_device_ids=true | all-gather | bytes 25344 | tf_op jit(solution)/shard_map/all_gather | solution.py:110
  120.2 39.6 %all-gather.2 = bf16[1,3,4096]{2,1,0:T(4,128)(2,1)S(1)} all-gather(bf16[1,3,128]{2,1,0:T(4,128)(2,1)S(1)} %copy.59), channel_id=4, replica_groups=mesh['tgt'=32,'src'=8] {'tgt'}, dimensions={2}, use_global_device_ids=true | all-gather | bytes 25344 | tf_op jit(solution)/shard_map/all_gather | solution.py:110
  159.8 36.7 %all-gather.3 = bf16[1,3,4096]{2,1,0:T(4,128)(2,1)S(1)} all-gather(bf16[1,3,128]{2,1,0:T(4,128)(2,1)S(1)} %copy.60), channel_id=5, replica_groups=mesh['tgt'=32,'src'=8] {'tgt'}, dimensions={2}, use_global_device_ids=true | all-gather | bytes 25344 | tf_op jit(solution)/shard_map/all_gather | solution.py:110
  196.5 78.8 %while.56 = (s32[]{:T(128)}, f32[512,128]{0,1:T(8,128)S(1)}, bf16[3,512]{1,0:T(4,128)(2,1)S(1)}, bf16[3,4096]{1,0:T(4,128)(2,1)S(1)}, bf16[128,4096]{1,0:T(8,128...) while((s32[]{:T(128)}, f32[512,128]{0,1:T(8,128)S(1)}, bf16[3,512]{1,0:T(4,128)(2,1)S(1)}, ...), condition=%wide.region_3.4_spmd.clone, body=%wide.region_2.3_spmd.clone.sunk | while | flops 281283584 | bytes 2713769 | solution.py:78
  196.7 9.7 %fusion.110 = f32[512,128]{0,1:T(8,128)S(1)} fusion(f32[1024]{0:T(1024)S(1)} %bitcast.278, f32[512]{0:T(512)S(1)} %bitcast.304, f32[1024]{0:T(1024)S(1)} %bitcast.280, f32[512]{0:T(512)S(1)} %bitcast.302, f32[1024]{0:T(1024)S(1)} %bitcast.276, f32[512]{0:T(512)S(1)} %bitcast.300, bf16[128,4096]{1,0:T(8,128)(2,1)} %get-tuple-element.859, ...), kind=kOutput, calls=%fused_computation.79.clone.1 | convolution fusion | flops 140509184 | bytes 542724 | tf_op jit(solution)/shard_map/while/body/eval_jaxpr/dot_general | solution.py:39
  216.3 9.7 %fusion.110 = f32[512,128]{0,1:T(8,128)S(1)} fusion(f32[1024]{0:T(1024)S(1)} %bitcast.278, f32[512]{0:T(512)S(1)} %bitcast.304, f32[1024]{0:T(1024)S(1)} %bitcast.280, f32[512]{0:T(512)S(1)} %bitcast.302, f32[1024]{0:T(1024)S(1)} %bitcast.276, f32[512]{0:T(512)S(1)} %bitcast.300, bf16[128,4096]{1,0:T(8,128)(2,1)} %get-tuple-element.859, ...), kind=kOutput, calls=%fused_computation.79.clone.1 | convolution fusion | flops 140509184 | bytes 542724 | tf_op jit(solution)/shard_map/while/body/eval_jaxpr/dot_general | solution.py:39
  235.8 9.7 %fusion.110 = f32[512,128]{0,1:T(8,128)S(1)} fusion(f32[1024]{0:T(1024)S(1)} %bitcast.278, f32[512]{0:T(512)S(1)} %bitcast.304, f32[1024]{0:T(1024)S(1)} %bitcast.280, f32[512]{0:T(512)S(1)} %bitcast.302, f32[1024]{0:T(1024)S(1)} %bitcast.276, f32[512]{0:T(512)S(1)} %bitcast.300, bf16[128,4096]{1,0:T(8,128)(2,1)} %get-tuple-element.859, ...), kind=kOutput, calls=%fused_computation.79.clone.1 | convolution fusion | flops 140509184 | bytes 542724 | tf_op jit(solution)/shard_map/while/body/eval_jaxpr/dot_general | solution.py:39
  255.4 9.7 %fusion.110 = f32[512,128]{0,1:T(8,128)S(1)} fusion(f32[1024]{0:T(1024)S(1)} %bitcast.278, f32[512]{0:T(512)S(1)} %bitcast.304, f32[1024]{0:T(1024)S(1)} %bitcast.280, f32[512]{0:T(512)S(1)} %bitcast.302, f32[1024]{0:T(1024)S(1)} %bitcast.276, f32[512]{0:T(512)S(1)} %bitcast.300, bf16[128,4096]{1,0:T(8,128)(2,1)} %get-tuple-element.859, ...), kind=kOutput, calls=%fused_computation.79.clone.1 | convolution fusion | flops 140509184 | bytes 542724 | tf_op jit(solution)/shard_map/while/body/eval_jaxpr/dot_general | solution.py:39
  275.3 78.1 %while.53 = (s32[]{:T(128)}, f32[512,128]{0,1:T(8,128)S(1)}, bf16[3,512]{1,0:T(4,128)(2,1)S(1)}, bf16[3,4096]{1,0:T(4,128)(2,1)S(1)}, bf16[128,4096]{1,0:T(8,128...) while((s32[]{:T(128)}, f32[512,128]{0,1:T(8,128)S(1)}, bf16[3,512]{1,0:T(4,128)(2,1)S(1)}, ...), condition=%wide.region_7.8_spmd, body=%wide.region_6.7_spmd.sunk | while | flops 281218048 | bytes 2713759 | solution.py:78
  275.4 9.7 %fusion.92 = f32[512,128]{0,1:T(8,128)S(1)} fusion(f32[1024]{0:T(1024)S(1)} %bitcast.284, f32[512]{0:T(512)S(1)} %bitcast.310, f32[1024]{0:T(1024)S(1)} %bitcast.286, f32[512]{0:T(512)S(1)} %bitcast.308, f32[1024]{0:T(1024)S(1)} %bitcast.282, f32[512]{0:T(512)S(1)} %bitcast.306, bf16[128,4096]{1,0:T(8,128)(2,1)} %get-tuple-element.886, ...), kind=kOutput, calls=%fused_computation.28.clone.1 | convolution fusion | flops 140509184 | bytes 542724 | tf_op jit(solution)/shard_map/while/body/eval_jaxpr/dot_general | solution.py:39
  294.9 9.7 %fusion.92 = f32[512,128]{0,1:T(8,128)S(1)} fusion(f32[1024]{0:T(1024)S(1)} %bitcast.284, f32[512]{0:T(512)S(1)} %bitcast.310, f32[1024]{0:T(1024)S(1)} %bitcast.286, f32[512]{0:T(512)S(1)} %bitcast.308, f32[1024]{0:T(1024)S(1)} %bitcast.282, f32[512]{0:T(512)S(1)} %bitcast.306, bf16[128,4096]{1,0:T(8,128)(2,1)} %get-tuple-element.886, ...), kind=kOutput, calls=%fused_computation.28.clone.1 | convolution fusion | flops 140509184 | bytes 542724 | tf_op jit(solution)/shard_map/while/body/eval_jaxpr/dot_general | solution.py:39
  314.5 9.7 %fusion.92 = f32[512,128]{0,1:T(8,128)S(1)} fusion(f32[1024]{0:T(1024)S(1)} %bitcast.284, f32[512]{0:T(512)S(1)} %bitcast.310, f32[1024]{0:T(1024)S(1)} %bitcast.286, f32[512]{0:T(512)S(1)} %bitcast.308, f32[1024]{0:T(1024)S(1)} %bitcast.282, f32[512]{0:T(512)S(1)} %bitcast.306, bf16[128,4096]{1,0:T(8,128)(2,1)} %get-tuple-element.886, ...), kind=kOutput, calls=%fused_computation.28.clone.1 | convolution fusion | flops 140509184 | bytes 542724 | tf_op jit(solution)/shard_map/while/body/eval_jaxpr/dot_general | solution.py:39
  334.0 9.7 %fusion.92 = f32[512,128]{0,1:T(8,128)S(1)} fusion(f32[1024]{0:T(1024)S(1)} %bitcast.284, f32[512]{0:T(512)S(1)} %bitcast.310, f32[1024]{0:T(1024)S(1)} %bitcast.286, f32[512]{0:T(512)S(1)} %bitcast.308, f32[1024]{0:T(1024)S(1)} %bitcast.282, f32[512]{0:T(512)S(1)} %bitcast.306, bf16[128,4096]{1,0:T(8,128)(2,1)} %get-tuple-element.886, ...), kind=kOutput, calls=%fused_computation.28.clone.1 | convolution fusion | flops 140509184 | bytes 542724 | tf_op jit(solution)/shard_map/while/body/eval_jaxpr/dot_general | solution.py:39
  353.5 78.3 %while.54 = (s32[]{:T(128)}, f32[512,128]{0,1:T(8,128)S(1)}, bf16[3,512]{1,0:T(4,128)(2,1)S(1)}, bf16[3,4096]{1,0:T(4,128)(2,1)S(1)}, bf16[128,4096]{1,0:T(8,128...) while((s32[]{:T(128)}, f32[512,128]{0,1:T(8,128)S(1)}, bf16[3,512]{1,0:T(4,128)(2,1)S(1)}, ...), condition=%wide.region_11.12_spmd, body=%wide.region_10.11_spmd.sunk | while | flops 281218048 | bytes 2713759 | solution.py:78
  373.3 9.7 %fusion.98 = f32[512,128]{0,1:T(8,128)S(1)} fusion(f32[1024]{0:T(1024)S(1)} %bitcast.290, f32[512]{0:T(512)S(1)} %bitcast.316, f32[1024]{0:T(1024)S(1)} %bitcast.292, f32[512]{0:T(512)S(1)} %bitcast.314, f32[1024]{0:T(1024)S(1)} %bitcast.288, f32[512]{0:T(512)S(1)} %bitcast.312, bf16[128,4096]{1,0:T(8,128)(2,1)} %get-tuple-element.913, ...), kind=kOutput, calls=%fused_computation.45.clone.1 | convolution fusion | flops 140509184 | bytes 542724 | tf_op jit(solution)/shard_map/while/body/eval_jaxpr/dot_general | solution.py:39
  392.8 9.7 %fusion.98 = f32[512,128]{0,1:T(8,128)S(1)} fusion(f32[1024]{0:T(1024)S(1)} %bitcast.290, f32[512]{0:T(512)S(1)} %bitcast.316, f32[1024]{0:T(1024)S(1)} %bitcast.292, f32[512]{0:T(512)S(1)} %bitcast.314, f32[1024]{0:T(1024)S(1)} %bitcast.288, f32[512]{0:T(512)S(1)} %bitcast.312, bf16[128,4096]{1,0:T(8,128)(2,1)} %get-tuple-element.913, ...), kind=kOutput, calls=%fused_computation.45.clone.1 | convolution fusion | flops 140509184 | bytes 542724 | tf_op jit(solution)/shard_map/while/body/eval_jaxpr/dot_general | solution.py:39
  412.3 9.7 %fusion.98 = f32[512,128]{0,1:T(8,128)S(1)} fusion(f32[1024]{0:T(1024)S(1)} %bitcast.290, f32[512]{0:T(512)S(1)} %bitcast.316, f32[1024]{0:T(1024)S(1)} %bitcast.292, f32[512]{0:T(512)S(1)} %bitcast.314, f32[1024]{0:T(1024)S(1)} %bitcast.288, f32[512]{0:T(512)S(1)} %bitcast.312, bf16[128,4096]{1,0:T(8,128)(2,1)} %get-tuple-element.913, ...), kind=kOutput, calls=%fused_computation.45.clone.1 | convolution fusion | flops 140509184 | bytes 542724 | tf_op jit(solution)/shard_map/while/body/eval_jaxpr/dot_general | solution.py:39
  431.8 91.2 %while.55 = (s32[]{:T(128)}, f32[512,128]{0,1:T(8,128)S(1)}, bf16[3,512]{1,0:T(4,128)(2,1)S(1)}, bf16[3,4096]{1,0:T(4,128)(2,1)S(1)}, bf16[128,4096]{1,0:T(8,128...) while((s32[]{:T(128)}, f32[512,128]{0,1:T(8,128)S(1)}, bf16[3,512]{1,0:T(4,128)(2,1)S(1)}, ...), condition=%wide.region_15.16_spmd, body=%wide.region_14.15_spmd.sunk | while | flops 281218048 | bytes 2713759 | solution.py:78
  445.0 9.7 %fusion.104 = f32[512,128]{0,1:T(8,128)S(1)} fusion(f32[1024]{0:T(1024)S(1)} %bitcast.296, f32[512]{0:T(512)S(1)} %bitcast.322, f32[1024]{0:T(1024)S(1)} %bitcast.298, f32[512]{0:T(512)S(1)} %bitcast.320, f32[1024]{0:T(1024)S(1)} %bitcast.294, f32[512]{0:T(512)S(1)} %bitcast.318, bf16[128,4096]{1,0:T(8,128)(2,1)} %get-tuple-element.940, ...), kind=kOutput, calls=%fused_computation.62.clone.1 | convolution fusion | flops 140509184 | bytes 542724 | tf_op jit(solution)/shard_map/while/body/eval_jaxpr/dot_general | solution.py:39
  464.5 9.7 %fusion.104 = f32[512,128]{0,1:T(8,128)S(1)} fusion(f32[1024]{0:T(1024)S(1)} %bitcast.296, f32[512]{0:T(512)S(1)} %bitcast.322, f32[1024]{0:T(1024)S(1)} %bitcast.298, f32[512]{0:T(512)S(1)} %bitcast.320, f32[1024]{0:T(1024)S(1)} %bitcast.294, f32[512]{0:T(512)S(1)} %bitcast.318, bf16[128,4096]{1,0:T(8,128)(2,1)} %get-tuple-element.940, ...), kind=kOutput, calls=%fused_computation.62.clone.1 | convolution fusion | flops 140509184 | bytes 542724 | tf_op jit(solution)/shard_map/while/body/eval_jaxpr/dot_general | solution.py:39
  484.1 9.7 %fusion.104 = f32[512,128]{0,1:T(8,128)S(1)} fusion(f32[1024]{0:T(1024)S(1)} %bitcast.296, f32[512]{0:T(512)S(1)} %bitcast.322, f32[1024]{0:T(1024)S(1)} %bitcast.298, f32[512]{0:T(512)S(1)} %bitcast.320, f32[1024]{0:T(1024)S(1)} %bitcast.294, f32[512]{0:T(512)S(1)} %bitcast.318, bf16[128,4096]{1,0:T(8,128)(2,1)} %get-tuple-element.940, ...), kind=kOutput, calls=%fused_computation.62.clone.1 | convolution fusion | flops 140509184 | bytes 542724 | tf_op jit(solution)/shard_map/while/body/eval_jaxpr/dot_general | solution.py:39
  503.6 9.7 %fusion.104 = f32[512,128]{0,1:T(8,128)S(1)} fusion(f32[1024]{0:T(1024)S(1)} %bitcast.296, f32[512]{0:T(512)S(1)} %bitcast.322, f32[1024]{0:T(1024)S(1)} %bitcast.298, f32[512]{0:T(512)S(1)} %bitcast.320, f32[1024]{0:T(1024)S(1)} %bitcast.294, f32[512]{0:T(512)S(1)} %bitcast.318, bf16[128,4096]{1,0:T(8,128)(2,1)} %get-tuple-element.940, ...), kind=kOutput, calls=%fused_computation.62.clone.1 | convolution fusion | flops 140509184 | bytes 542724 | tf_op jit(solution)/shard_map/while/body/eval_jaxpr/dot_general | solution.py:39
  524.0 71.4 %all-reduce.2.cloned.1.call-done = f32[512,128]{1,0:T(8,128)} async-done(((f32[512,128]{1,0:T(8,128)}), f32[512,128]{1,0:T(8,128)}) %all-reduce.2.cloned.1.call-update) | async-done | bytes 262160 | tf_op jit(solution)/shard_map/psum | solution.py:114
  (213 shorter events, 212.5 us)
Async XLA Ops:
  6.5 190.0 %all-gather.9.cloned.1.call-start = ((), (), s32[]{:S(2)}) async-start(), calls=%async_computation | async-start | bytes 1081344 | tf_op jit(solution)/shard_map/all_gather | solution.py:111
  17.7 5.0 copy-start.6
  17.7 5.0 copy-start.7
  17.7 5.0 copy-start.8
  17.7 5.1 copy-start.5
  23.6 251.7 %all-gather.11.cloned.1.call-start = ((), (), s32[]{:S(2)}) async-start(), calls=%async_computation.1 | async-start | bytes 1081344 | tf_op jit(solution)/shard_map/all_gather | solution.py:111
  26.8 326.6 %all-gather.13.cloned.1.call-start = ((), (), s32[]{:S(2)}) async-start(), calls=%async_computation.2 | async-start | bytes 1081344 | tf_op jit(solution)/shard_map/all_gather | solution.py:111
  32.7 4.5 copy-start.4
  33.0 163.5 %copy-start = (bf16[3,512]{1,0:T(4,128)(2,1)S(1)}, bf16[3,512]{1,0:T(4,128)(2,1)}, u32[]{:S(2)}) copy-start(bf16[3,512]{1,0:T(4,128)(2,1)} %param.20) | copy-start | bytes 9220
  33.9 397.9 %all-gather.15.cloned.1.call-start = ((), (), s32[]{:S(2)}) async-start(), calls=%async_computation.3 | async-start | bytes 1081344 | tf_op jit(solution)/shard_map/all_gather | solution.py:111
  37.2 558.2 %all-reduce.2.cloned.1.call-start = ((), (), s32[]{:S(2)}) async-start(), calls=%async_computation.4 | async-start | bytes 524288 | tf_op jit(solution)/shard_map/psum | solution.py:114
  431.8 92.1 %copy-start.9 = (f32[512]{0:T(512)S(1)}, f32[512]{0:T(512)}, u32[]{:S(2)}) copy-start(f32[512]{0:T(512)} %param.21) | copy-start | bytes 6148
  431.8 92.1 %copy-start.3 = (f32[8,512]{1,0:T(8,128)S(1)}, f32[8,512]{1,0:T(8,128)}, u32[]{:S(2)}) copy-start(f32[8,512]{1,0:T(8,128)} %param.30) | copy-start | bytes 49156
  523.1 85.3 %copy-start.2 = (s32[8]{0:T(128)S(1)}, s32[8]{0:T(128)}, u32[]{:S(2)}) copy-start(s32[8]{0:T(128)} %param.31) | copy-start | bytes 100
  595.4 23.9 %copy-start.1 = (f32[512,128]{1,0:T(8,128)S(1)}, f32[512,128]{1,0:T(8,128)}, u32[]{:S(2)}) copy-start(f32[512,128]{1,0:T(8,128)} %all-reduce.2.cloned.1.call-done) | copy-start | bytes 786436
  596.6 22.7 %collective-permute-start.1 = (f32[8,128]{1,0:T(8,128)S(1)}, f32[8,128]{1,0:T(8,128)S(1)}, u32[]{:S(2)}, u32[]{:S(2)}) collective-permute-start(f32[8,128]{1,0:T(8,128)S(1)} %get-tuple-element.560), channel_id=1, source_target_pairs={{8,0},{16,8},{24,16},{32,24},{40,32},{48,40},{56,48},{64,56},{72,6... | collective-permute-start | bytes 12296 | tf_op jit(solution)/shard_map/ppermute | solution.py:23
  604.1 15.2 %collective-permute-start = (f32[8,128]{1,0:T(8,128)S(1)}, f32[8,128]{1,0:T(8,128)S(1)}, u32[]{:S(2)}, u32[]{:S(2)}) collective-permute-start(f32[8,128]{1,0:T(8,128)S(1)} %get-tuple-element.559), channel_id=1, source_target_pairs={{0,8},{8,16},{16,24},{24,32},{32,40},{40,48},{48,56},{56,64},{64,7... | collective-permute-start | bytes 12296 | tf_op jit(solution)/shard_map/ppermute | solution.py:20
Sparse Core Ops, SparseCore 0:
  23.7 76.4 all-gather.8
  102.7 70.0 all-gather.10
  175.4 69.8 all-gather.12
  247.7 69.9 all-gather.14
  524.1 71.3 all-reduce.1
where the time goes:
time: 635 us; the launch traced here: 628 us
  matrix products  309 us (49%)
  blocking collectives  159 us (25%)
  waiting for transfers between devices  71.6 us (11%)
  local copies, waits for them, and re-layouts  28.2 us (4%)
  between operations  24.2 us (4%)
  loops' own time  15.1 us (2%)
  starting transfers between devices  11.9 us (2%)
  other arithmetic  8.44 us (1%)
    all_gather x4, blocking collectives, per_device(): lax.all_gather(src_points[section], 'tgt', axis=1, tiled=True)  159 us
    dot_general x16, matrix products, kernel_terms(): lax.dot_general(kernel_im, density, dims, preferred_element_type=jnp.floa...  155 us
    dot_general x16, matrix products, kernel_terms(): lax.dot_general(kernel_re, density, dims, preferred_element_type=jnp.floa...  154 us
    psum x1, waiting for transfers between devices, per_device(): total = lax.psum(partial_value, 'src')  71.4 us
    another operation x4, loops' own time, add_kernel(): return lax.fori_loop(0, width // block_size, step_fn, carried)  15.1 us
    gather x12, local copies, waits for them, and re-layouts, block_density(): scaled = basis_rows[basis_index] * weights_ctrl[control_index]  14.7 us
  transfers between devices with their start and end apart: 7, of which 1 were waited for; matrix products, arithmetic and copies ran while one was open for 39% of the time, Pallas kernels for 0%

commit v1 on v0

v1 whole, which is shorter than its diff:
```python
import functools
import math

import jax
import jax.numpy as jnp
import numpy as np
from jax import lax
from jax.experimental import pallas as pl
from jax.experimental.pallas import tpu as pltpu
from jax.sharding import Mesh, PartitionSpec as P

HALO = 8
WAVE = 8.0
SMOOTH = 0.0025
TURN = WAVE / (2.0 * math.pi)
TURN_SQ = TURN * TURN

TGT = ("z", "yh", "core")
SRC = ("yl", "x")

SIN_POLY = ()
COS_POLY = ()


def minimax(func, terms, odd):
    nodes = 0.25 + 0.25 * np.cos(np.linspace(0.0, np.pi, 2001))
    nodes = nodes[nodes > 1e-6]
    scale = nodes if odd else np.ones_like(nodes)
    basis = np.stack([nodes ** (2 * k) for k in range(terms)], 1)
    value = func(nodes) / scale
    weight = np.ones_like(nodes)
    for _ in range(60):
        rows = scale * weight
        coef = np.linalg.lstsq(basis * rows[:, None], value * rows, rcond=None)[0]
        error = np.abs((basis @ coef - value) * scale)
        weight = weight * np.sqrt(1e-12 + error / error.max())
        weight = weight / weight.mean()
    return tuple(float(np.float32(c)) for c in coef)


SIN_POLY = minimax(lambda f: math.sqrt(2.0) * np.sin(np.pi * f), 3, True)
COS_POLY = minimax(lambda f: math.sqrt(2.0) * np.cos(np.pi * f), 4, False)


def horner(z, coef):
    value = coef[-1]
    for c in coef[-2::-1]:
        value = value * z + c
    return value


def split3(value):
    high = value.astype(jnp.bfloat16).astype(jnp.float32)
    rest = value - high
    mid = rest.astype(jnp.bfloat16).astype(jnp.float32)
    return high, mid, rest - mid


def payload_kernel(factor_ref, points_ref, weight_ref, basis_ref, span_ref, patch_ref, cweight_ref, coef_ref, out_ref):
    rounds = points_ref.shape[0]
    controls = cweight_ref.shape[1]
    count = points_ref.shape[2]
    label = lax.broadcasted_iota(jnp.int32, (controls, count), 0)
    pieces = []
    for s in range(rounds):
        span = span_ref[s : s + 1, :]
        patch = patch_ref[s : s + 1, :]
        column = jnp.transpose(jnp.broadcast_to(cweight_ref[s : s + 1, :], (8, controls)))[:, 0:1]
        scaled = []
        for a in range(3):
            picked = jnp.where(label == span + a, column, 0.0)
            scaled.append(basis_ref[s, a : a + 1, :] * jnp.sum(picked, axis=0, keepdims=True))
        denom = scaled[0] + scaled[1] + scaled[2]
        fre = jnp.zeros((1, count), jnp.float32)
        fim = jnp.zeros((1, count), jnp.float32)
        for p in range(factor_ref.shape[2]):
            fre = jnp.where(patch == p, factor_ref[s, 0, p], fre)
            fim = jnp.where(patch == p, factor_ref[s, 1, p], fim)
        weight = weight_ref[s : s + 1, :] / denom
        terms = [value * (weight * fre) for value in scaled] + [value * (weight * fim) for value in scaled]
        high = [t.astype(jnp.bfloat16).astype(jnp.float32) for t in terms]
        low = [t - h for t, h in zip(terms, high)]
        rows = [points_ref[s].astype(jnp.float32), span.astype(jnp.float32)] + high + low
        pieces.append(jnp.concatenate(rows, axis=0))
    coef = jnp.concatenate([jnp.transpose(coef_ref[s].astype(jnp.float32)) for s in range(rounds)], axis=0)
    whole = jnp.concatenate([coef] + pieces, axis=0).astype(jnp.bfloat16)
    for copy in range(out_ref.shape[0]):
        out_ref[copy] = whole


def source_payload(copies, factor, points, weight, basis, span, patch, cweight, coef):
    rounds, fields, controls = coef.shape
    count = points.shape[2]
    rows = rounds * controls + 16 * rounds
    vmem = pl.BlockSpec(memory_space=pltpu.VMEM)
    return pl.pallas_call(
        payload_kernel,
        in_specs=[pl.BlockSpec(memory_space=pltpu.SMEM)] + [vmem] * 7,
        out_specs=vmem,
        out_shape=jax.ShapeDtypeStruct((copies, rows, count), jnp.bfloat16),
        name="payload",
    )(factor, points, weight, basis, span, patch, cweight, coef)


def density_kernel(rounds, controls, gathered_ref, density_ref, feature_ref):
    count = gathered_ref.shape[2]
    base = rounds * controls
    label = lax.broadcasted_iota(jnp.int32, (controls, count), 0).astype(jnp.float32)
    ones = jnp.ones((3, count), jnp.float32)
    zero = jnp.zeros((1, count), jnp.float32)
    for z in range(gathered_ref.shape[0]):
        for s in range(rounds):
            block = z * rounds + s
            rows = gathered_ref[z, base + 16 * s : base + 16 * s + 16, :].astype(jnp.float32)
            pos, span = rows[0:3], rows[3:4]
            masks = [label == span + float(a) for a in range(3)]
            spread = []
            for part in range(4):
                value = jnp.zeros((controls, count), jnp.float32)
                for a in range(3):
                    row = rows[4 + 3 * part + a : 5 + 3 * part + a]
                    value = jnp.where(masks[a], row, value)
                spread.append(value)
            spread = jnp.concatenate(spread, axis=0).astype(jnp.bfloat16)
            plain = gathered_ref[z, s * controls : (s + 1) * controls, :]
            half = plain.shape[1] // 2
            turned = jnp.concatenate([-plain[:, half:], plain[:, :half]], axis=1)
            matrix = jnp.concatenate([plain, turned, plain, turned], axis=0)
            value = lax.dot_general(
                spread, matrix, (((0,), (0,)), ((), ())), preferred_element_type=jnp.float32
            )
            density_ref[block * count : (block + 1) * count, :] = value.astype(jnp.bfloat16)
            norm = pos[0:1] * pos[0:1] + pos[1:2] * pos[1:2] + pos[2:3] * pos[2:3]
            feature = jnp.concatenate([pos, pos, pos, ones, *split3(norm * TURN_SQ), zero], axis=0)
            feature_ref[:, block * count : (block + 1) * count] = feature.astype(jnp.bfloat16)


def source_density(gathered, rounds, controls):
    total = gathered.shape[0] * rounds * gathered.shape[2]
    vmem = pl.BlockSpec(memory_space=pltpu.VMEM)
    return pl.pallas_call(
        functools.partial(density_kernel, rounds, controls),
        in_specs=[vmem],
        out_specs=[vmem, vmem],
        out_shape=[
            jax.ShapeDtypeStruct((total, gathered.shape[2]), jnp.bfloat16),
            jax.ShapeDtypeStruct((16, total), jnp.bfloat16),
        ],
        name="density",
    )(gathered)


def terms_kernel(width, has_start, *refs):
    if has_start:
        target_ref, feature_ref, density_ref, start_ref, out_ref, side_ref, total_ref = refs
    else:
        target_ref, feature_ref, density_ref, out_ref, side_ref, total_ref = refs
    rows = out_ref.shape[0]
    step = pl.program_id(0)

    @pl.when(step == 0)
    def _():
        pos = target_ref[...]
        norm = pos[0:1] * pos[0:1] + pos[1:2] * pos[1:2] + pos[2:3] * pos[2:3] + SMOOTH
        scaled = [p for t in [split3(pos[0:3] * (-2.0 * TURN_SQ))] for p in t]
        ones = jnp.ones((3, pos.shape[1]), jnp.float32)
        side = jnp.concatenate(scaled + [*split3(norm * TURN_SQ), ones, jnp.zeros_like(norm)], axis=0)
        side_ref[...] = jnp.transpose(side)[:rows].astype(jnp.bfloat16)
        total_ref[...] = jnp.zeros_like(total_ref)

    side = side_ref[...]
    chunks = feature_ref.shape[1] // width

    def squared(q):
        return jnp.dot(side, feature_ref[:, q * width : (q + 1) * width], preferred_element_type=jnp.float32)

    def add(terms, q):
        total_ref[...] += jnp.dot(
            terms, density_ref[q * width : (q + 1) * width, :], preferred_element_type=jnp.float32
        )

    square = squared(0)
    ready = None
    for q in range(chunks):
        later = squared(q + 1) if q + 1 < chunks else None
        inverse = lax.rsqrt(square)
        turns = square * inverse
        part = turns - jnp.round(turns)
        z = part * part
        sine = part * horner(z, SIN_POLY)
        cosine = horner(z, COS_POLY)
        scaled = sine * inverse
        kre = (inverse - sine * scaled).astype(jnp.bfloat16)
        kim = (scaled * cosine).astype(jnp.bfloat16)
        terms = jnp.concatenate([kre, kim], axis=0)
        if ready is not None:
            add(ready, q - 1)
        ready, square = terms, later
    add(ready, chunks - 1)

    @pl.when(step == pl.num_programs(0) - 1)
    def _():
        plain = total_ref[:rows]
        other = total_ref[rows:]
        half = plain.shape[1] // 2
        out = plain + jnp.concatenate([-other[:, half:], other[:, :half]], axis=1)
        if has_start:
            out = out + start_ref[...]
        out_ref[...] = out


def kernel_sums(targets, rows, feature, density, start=None, step=1024, width=512):
    total, columns = density.shape
    whole = pl.BlockSpec((rows, columns), lambda i: (0, 0))
    in_specs = [
        pl.BlockSpec(targets.shape, lambda i: (0, 0)),
        pl.BlockSpec((16, step), lambda i: (0, i)),
        pl.BlockSpec((step, columns), lambda i: (i, 0)),
    ]
    args = [targets, feature, density]
    if start is not None:
        in_specs.append(whole)
        args.append(start)
    return pl.pallas_call(
        functools.partial(terms_kernel, width, start is not None),
        grid=(total // step,),
        in_specs=in_specs,
        out_specs=whole,
        out_shape=jax.ShapeDtypeStruct((rows, columns), jnp.float32),
        scratch_shapes=[pltpu.VMEM((rows, 16), jnp.bfloat16), pltpu.VMEM((2 * rows, columns), jnp.float32)],
        compiler_params=pltpu.CompilerParams(vmem_limit_bytes=40 << 20),
        cost_estimate=pl.CostEstimate(
            flops=rows * total * columns * 8, bytes_accessed=total * columns * 2, transcendentals=rows * total
        ),
        name="terms",
    )(*args)


def per_device(
    tgt_points, tgt_weight, src_points, src_weight, basis, span, patch, patch_factor, ctrl_weight, ctrl_coef, band, offsets
):
    rows = tgt_points.shape[1]
    rounds, columns, controls = ctrl_coef.shape
    zs = lax.axis_size("z")
    groups = lax.axis_size(SRC)
    blocks = lax.axis_size(TGT)

    w_high = lax.reduce_precision(tgt_weight, 8, 7)
    w_mid = lax.reduce_precision(tgt_weight - w_high, 8, 7)
    w_rows = jnp.stack([w_high, w_mid, tgt_weight - w_high - w_mid])
    side = jnp.concatenate([tgt_points, w_rows.astype(jnp.bfloat16), jnp.zeros((2, rows), jnp.bfloat16)], axis=0)
    forward = [(i, i + 1) for i in range(blocks - 1)]
    low = lax.ppermute(side, TGT, forward)
    high = lax.ppermute(side, TGT, [(b, a) for a, b in forward])
    span_rows = rows + 2 * HALO
    lanes = -(-span_rows // 128) * 128
    wide = jnp.concatenate(
        [low[:, rows - HALO :], side, high[:, :HALO], jnp.zeros((8, lanes - span_rows), jnp.bfloat16)], axis=1
    )
    swap = [(0, 1), (1, 0)]
    wide_peer = lax.ppermute(wide, "yh", swap)
    own_pos = wide.astype(jnp.float32)
    peer_pos = wide_peer.astype(jnp.float32)

    sent = source_payload(
        zs, patch_factor, src_points, src_weight, basis, span, patch, ctrl_weight, ctrl_coef
    )
    gathered = lax.all_to_all(sent, "z", split_axis=0, concat_axis=0, tiled=True)
    density, feature = source_density(gathered, rounds, controls)
    density2 = lax.ppermute(density, "core", swap)
    feature2 = lax.ppermute(feature, "core", swap)

    peer = kernel_sums(peer_pos, span_rows, feature, density)
    peer = kernel_sums(peer_pos, span_rows, feature2, density2, peer)
    arrived = lax.ppermute(peer, "yh", swap)
    own = kernel_sums(own_pos, span_rows, feature, density)
    own = kernel_sums(own_pos, span_rows, feature2, density2, own)
    own = own + arrived

    share = -(-span_rows // (8 * groups)) * 8
    own = jnp.pad(own, ((0, share * groups - span_rows), (0, 0))).reshape(groups, share, columns)
    shares = lax.all_to_all(own, SRC, split_axis=0, concat_axis=0, tiled=True)
    summed = jnp.sum(shares, axis=0)
    spread = jnp.broadcast_to(summed[None], (groups, share, columns))
    total = lax.all_to_all(spread, SRC, split_axis=0, concat_axis=0, tiled=True)
    total = total.reshape(groups * share, columns)[:span_rows]

    source_count = rounds * src_weight.shape[1] * blocks * groups
    scale = jnp.float32(TURN / math.sqrt(source_count))
    tail = own_pos[3:6, :span_rows]
    weight = (tail[0] + tail[1]) + tail[2]
    padded = total * (weight * scale)[:, None]
    potential = lax.slice_in_dim(padded, HALO, HALO + rows, axis=0)
    shell_field = potential
    for diag in range(band.shape[0]):
        shifted = lax.dynamic_slice_in_dim(padded, HALO + offsets[diag], rows, 0)
        shell_field = shell_field + band[diag][:, None] * shifted
    return shell_field


def solution(mesh):
    mesh = Mesh(mesh.devices.reshape(8, 2, 2, 2, 4), ("z", "yh", "core", "yl", "x"))
    both = TGT + SRC
    in_specs = (
        P(None, TGT),
        P(TGT),
        P(None, None, both),
        P(None, both),
        P(None, None, both),
        P(None, both),
        P(None, both),
        P(None, None, both),
        P(None, both),
        P(None, None, both),
        P(None, TGT),
        P(),
    )
    return jax.shard_map(
        per_device, mesh=mesh, in_specs=in_specs, out_specs=P(TGT, None), check_vma=False
    )
```

time: 635 us -> 115 us (0.18)
  matrix products: 309 us -> 0 us
  blocking collectives: 159 us -> 22.6 us
  waiting for transfers between devices: 71.6 us -> 8.36 us
  Pallas kernels: 0 us -> 35.7 us
  local copies, waits for them, and re-layouts: 28.2 us -> 7 us
  starting transfers between devices: 11.9 us -> 27.9 us
  loops' own time: 15.1 us -> 0 us
  between operations: 24.2 us -> 10.2 us
  other arithmetic: 8.44 us -> 1.64 us
    dot_general x32 -> x0, matrix products: 309 us -> none  [the longest x16 155 us: kernel_terms(): lax.dot_general(kernel_im, density, dims, preferred_element_type=jnp.floa...]
    all_gather x4 -> x0, blocking collectives: 159 us -> none  [per_device(): lax.all_gather(src_points[section], 'tgt', axis=1, tiled=True)]
    psum x1 -> x0, waiting for transfers between devices: 71.4 us -> none  [per_device(): total = lax.psum(partial_value, 'src')]
    pallas_call x0 -> x6, Pallas kernels: none -> 35.7 us  [the longest x4 31 us: kernel_sums(): pl.pallas_call(functools.partial(terms_kernel, width, start is not None),...]
    gather x36 -> x0, local copies, waits for them, and re-layouts: 24.6 us -> none  [the longest x12 14.7 us: block_density(): scaled = basis_rows[basis_index] * weights_ctrl[control_index]]
    all_to_all x0 -> x1, blocking collectives: none -> 22.6 us  [per_device(): lax.all_to_all(sent, 'z', split_axis=0, concat_axis=0, tiled=True)]
    another operation x4 -> x0, loops' own time: 15.1 us -> none  [add_kernel(): return lax.fori_loop(0, width // block_size, step_fn, carried)]
    all_to_all x0 -> x2, starting transfers between devices: none -> 10.4 us  [the longest x1 5.27 us: per_device(): total = lax.all_to_all(spread, SRC, split_axis=0, concat_axis=0, tiled=True)]
  transfers between devices with their start and end apart: 7 -> 8, of which waited for: 1 -> 3; matrix products, arithmetic and copies ran while one was open for 39% -> 1% of each run, Pallas kernels for 0% -> 20%
where the time goes in v1:
time: 115 us; the launch traced here: 114 us
  Pallas kernels  35.7 us (31%)
  starting transfers between devices  27.9 us (24%)
  blocking collectives  22.6 us (20%)
  between operations  10.2 us (9%)
  waiting for transfers between devices  8.36 us (7%)
  local copies, waits for them, and re-layouts  7 us (6%)
  other arithmetic  1.64 us (1%)
    pallas_call x4, Pallas kernels, kernel_sums(): pl.pallas_call(functools.partial(terms_kernel, width, start is not None),...  31 us
    all_to_all x1, blocking collectives, per_device(): lax.all_to_all(sent, 'z', split_axis=0, concat_axis=0, tiled=True)  22.6 us
    all_to_all x1, waiting for transfers between devices, per_device(): total = lax.all_to_all(spread, SRC, split_axis=0, concat_axis=0, tiled=True)  6.62 us
    all_to_all x1, starting transfers between devices, per_device(): total = lax.all_to_all(spread, SRC, split_axis=0, concat_axis=0, tiled=True)  5.27 us
    ppermute x1, starting transfers between devices, per_device(): low = lax.ppermute(side, TGT, forward)  5.14 us
    all_to_all x1, starting transfers between devices, per_device(): shares = lax.all_to_all(own, SRC, split_axis=0, concat_axis=0, tiled=True)  5.14 us
    unnamed x19, local copies, waits for them, and re-layouts  4.66 us
    ppermute x1, starting transfers between devices, per_device(): wide_peer = lax.ppermute(wide, 'yh', swap)  3.85 us
  transfers between devices with their start and end apart: 8, of which 3 were waited for; matrix products, arithmetic and copies ran while one was open for 1% of the time, Pallas kernels for 20%

profile of v1, /device:TPU:1, one launch (start us, length us, event | category | flops | bytes accessed | tf_op | source)
XLA Modules:
  0.0 113.5 jit_solution(11931344065475009084)
XLA Ops:
  0.0 1.3 %copy.13.points_ref = bf16[4,3,128]{2,1,0:T(4,128)(2,1)} copy(bf16[4,3,128]{2,0,1:T(4,128)(2,1)} %param.14) | data formatting | bytes 6144 | tf_op args[2]
  1.9 1.5 %copy.15.coef_ref = bf16[4,128,32]{2,1,0:T(8,128)(2,1)} copy(bf16[4,128,32]{1,2,0:T(8,128)(2,1)} %param.21) | data formatting | bytes 65536 | tf_op args[9]
  3.4 2.0 %payload.1 = bf16[8,192,128]{2,1,0:T(8,128)(2,1)} custom-call(f32[4,2,4]{2,1,0:T(2,128)} %factor_ref.1, bf16[4,3,128]{2,1,0:T(4,128)(2,1)} %copy.13.points_ref, f32[4,128]{1,0:T(4,128)} %weight_ref.1, f32[4,3,128]{2,1,0:T(4,128)} %copy.14.basis_ref, s32[4,128]{1,0:T(4,128)} %span_ref.1, s32[4,128]{1,0:T(4,128)} %patch_ref.1, f32[4,32]{1,0:T(4,128)} %cweight_ref.1, ...), custom_call_target="tpu_custom_call" | custom-call | tf_op jit(solution)/shard_map/payload/pallas_call | solution.py:96
  5.4 22.6 %all_to_all.15.gathered_ref = bf16[8,192,128]{2,1,0:T(8,128)(2,1)} all-to-all(bf16[8,192,128]{2,1,0:T(8,128)(2,1)} %payload.1), channel_id=1, replica_groups=mesh['z'=8,'yh'=2,'core'=2,'yl'=2,'x'=4] {'z'}, dimensions={0} | all-to-all | bytes 786432 | tf_op jit(solution)/shard_map/all_to_all | solution.py:268
  28.0 2.8 %density.1 = (bf16[4096,128]{1,0:T(8,128)(2,1)}, bf16[16,4096]{1,0:T(8,128)(2,1)}) custom-call(bf16[8,192,128]{2,1,0:T(8,128)(2,1)} %all_to_all.15.gathered_ref), custom_call_target="tpu_custom_call" | custom-call | tf_op jit(solution)/shard_map/density/pallas_call | solution.py:141
  30.8 2.1 %collective-permute-start.3 = (bf16[4096,128]{1,0:T(8,128)(2,1)}, bf16[4096,128]{1,0:T(8,128)(2,1)S(1)}, u32[]{:S(2)}, u32[]{:S(2)}) collective-permute-start(bf16[4096,128]{1,0:T(8,128)(2,1)} %get-tuple-element.8.refs_2_), channel_id=1, source_target_pairs={{0,8},{8,0},{1,9},{9,1},{2,10},{10,2},{3,11},{11,3},{4,12},{12,4},... | collective-permute-start | bytes 3145736 | tf_op jit(solution)/shard_map/ppermute | solution.py:270
  33.0 1.9 %collective-permute-start.1 = (bf16[8,512]{1,0:T(8,128)(2,1)S(1)}, bf16[8,512]{1,0:T(8,128)(2,1)S(1)}, u32[]{:S(2)}, u32[]{:S(2)}) collective-permute-start(bf16[8,512]{1,0:T(8,128)(2,1)S(1)} %concatenate.7), channel_id=1, source_target_pairs={{8,0},{16,8},{24,16},{32,24},{40,32},{48,40},{56,48},{64,56},{72,6... | collective-permute-start | bytes 24584 | tf_op jit(solution)/shard_map/ppermute | solution.py:254
  35.0 5.1 %collective-permute-start = (bf16[8,512]{1,0:T(8,128)(2,1)S(1)}, bf16[8,512]{1,0:T(8,128)(2,1)S(1)}, u32[]{:S(2)}, u32[]{:S(2)}) collective-permute-start(bf16[8,512]{1,0:T(8,128)(2,1)S(1)} %concatenate.7), channel_id=1, source_target_pairs={{0,8},{8,16},{16,24},{24,32},{32,40},{40,48},{48,56},{56,64},{64,7... | collective-permute-start | bytes 24584 | tf_op jit(solution)/shard_map/ppermute | solution.py:253
  40.2 0.7 collective-permute-done
  41.0 3.9 %collective-permute-start.4 = (bf16[8,640]{1,0:T(8,128)(2,1)S(1)}, bf16[8,640]{1,0:T(8,128)(2,1)S(1)}, u32[]{:S(2)}, u32[]{:S(2)}) collective-permute-start(bf16[8,640]{1,0:T(8,128)(2,1)S(1)} %get-tuple-element.10), channel_id=1, source_target_pairs={{0,16},{16,0},{1,17},{17,1},{2,18},{18,2},{3,19},{19,3},{4,20},{20... | collective-permute-start | bytes 30728 | tf_op jit(solution)/shard_map/ppermute | solution.py:261
  44.9 1.0 collective-permute-done.4
  45.9 1.0 collective-permute-start.2
  46.9 1.2 %copy-done = bf16[4096,128]{1,0:T(8,128)(2,1)S(1)} copy-done((bf16[4096,128]{1,0:T(8,128)(2,1)S(1)}, bf16[4096,128]{1,0:T(8,128)(2,1)}, u32[]{:S(2)}) %copy-start) | copy-done | bytes 1048600
  48.1 7.7 %terms.6.refs_3_ = f32[528,128]{1,0:T(8,128)S(1)} custom-call(f32[8,640]{1,0:T(8,128)S(1)} %convert_element_type.10.refs_0_, bf16[16,4096]{1,0:T(8,128)(2,1)S(1)} %copy-done.2, bf16[4096,128]{1,0:T(8,128)(2,1)S(1)} %copy-done), custom_call_target="tpu_custom_call" | custom-call | flops 2214592512 | bytes 1048576 | tf_op jit(solution)/shard_map/terms/pallas_call | solution.py:224
  55.9 7.8 %terms.7 = f32[528,128]{1,0:T(8,128)S(1)} custom-call(f32[8,640]{1,0:T(8,128)S(1)} %convert_element_type.10.refs_0_, bf16[16,4096]{1,0:T(8,128)(2,1)S(1)} %collective-permute-done.2.refs_1_, bf16[4096,128]{1,0:T(8,128)(2,1)S(1)} %collective-permute-done.3.refs_2_, f32[528,128]{1,0:T(8,128)S(1)} %terms.6.refs_3_), custom_call_target="tpu_custom_call" | custom-call | flops 2214592512 | bytes 1048576 | tf_op jit(solution)/shard_map/terms/pallas_call | solution.py:224
  63.6 3.5 %collective-permute-start.5 = (f32[528,128]{1,0:T(8,128)S(1)}, f32[528,128]{1,0:T(8,128)S(1)}, u32[]{:S(2)}, u32[]{:S(2)}) collective-permute-start(f32[528,128]{1,0:T(8,128)S(1)} %terms.7), channel_id=1, source_target_pairs={{0,16},{16,0},{1,17},{17,1},{2,18},{18,2},{3,19},{19,3},{4,20},{20... | collective-permute-start | bytes 811016 | tf_op jit(solution)/shard_map/ppermute | solution.py:275
  67.2 7.7 %terms.4.refs_3_ = f32[528,128]{1,0:T(8,128)S(1)} custom-call(f32[8,640]{1,0:T(8,128)S(1)} %get-tuple-element.9.refs_0_, bf16[16,4096]{1,0:T(8,128)(2,1)S(1)} %copy-done.2, bf16[4096,128]{1,0:T(8,128)(2,1)S(1)} %copy-done.1), custom_call_target="tpu_custom_call" | custom-call | flops 2214592512 | bytes 1048576 | tf_op jit(solution)/shard_map/terms/pallas_call | solution.py:224
  74.9 7.8 %terms.5 = f32[528,128]{1,0:T(8,128)S(1)} custom-call(f32[8,640]{1,0:T(8,128)S(1)} %get-tuple-element.9.refs_0_, bf16[16,4096]{1,0:T(8,128)(2,1)S(1)} %collective-permute-done.2.refs_1_, bf16[4096,128]{1,0:T(8,128)(2,1)S(1)} %collective-permute-done.3.refs_2_, f32[528,128]{1,0:T(8,128)S(1)} %terms.4.refs_3_), custom_call_target="tpu_custom_call" | custom-call | flops 2214592512 | bytes 1048576 | tf_op jit(solution)/shard_map/terms/pallas_call | solution.py:224
  82.7 0.7 pad.4
  83.5 5.1 %all-to-all-start.1 = ((f32[8,72,128]{2,1,0:T(8,128)}), f32[8,72,128]{2,1,0:T(8,128)S(1)}, u32[]{:S(2)}, u32[]{:S(2)}) async-start(f32[8,72,128]{2,1,0:T(8,128)} %bitcast), calls=%async_computation.1 | async-start | bytes 589824 | tf_op jit(solution)/shard_map/all_to_all | solution.py:282
  99.4 0.7 broadcast_in_dim.15
  100.1 5.3 %all-to-all-start.2 = ((f32[8,72,128]{2,1,0:T(8,128)}), f32[8,72,128]{2,1,0:T(8,128)S(1)}, u32[]{:S(2)}, u32[]{:S(2)}) async-start(f32[8,72,128]{2,1,0:T(8,128)} %broadcast_in_dim.15), calls=%async_computation.2 | async-start | bytes 589824 | tf_op jit(solution)/shard_map/all_to_all | solution.py:285
  105.4 6.6 %all-to-all-done.2 = f32[8,72,128]{2,1,0:T(8,128)S(1)} async-done(((f32[8,72,128]{2,1,0:T(8,128)}), f32[8,72,128]{2,1,0:T(8,128)S(1)}, u32[]{:S(2)}, u32[]{:S(2)}) %all-to-all-start.2) | async-done | bytes 294944 | tf_op jit(solution)/shard_map/all_to_all | solution.py:285
  112.2 1.3 %fusion.6 = f32[512,128]{1,0:T(8,128)} fusion(f32[528,128]{1,0:T(8,128)S(1)} %slice_multiply_fusion, s32[]{:T(128)S(6)} %select_n.31, s32[]{:T(128)S(6)} %select_n.30, s32[]{:T(128)S(6)} %select_n.29, s32[]{:T(128)S(6)} %select_n.28, s32[]{:T(128)S(6)} %select_n.27, s32[]{:T(128)S(6)} %select_n.26, s32[]{:T(128)S(6)} %select_n.25, s32[]{:T(128)S(6)} %select_n.24, ...), kind=kLoop, calls=%fused_computation.8 | loop fusion | flops 1048576 | bytes 2637856 | tf_op jit(solution)/shard_map/add | solution.py:297
  (39 shorter events, 1.8 us)
Async XLA Ops:
  0.0 1.3 %copy-start.5 = (f32[4,3,128]{2,0,1:T(4,128)S(1)}, f32[4,3,128]{2,0,1:T(4,128)}, u32[]{:S(2)}) copy-start(f32[4,3,128]{2,0,1:T(4,128)} %param.16) | copy-start | bytes 18436
  28.0 4.9 %copy-start.7 = (f32[512]{0:T(512)S(1)}, f32[512]{0:T(512)}, u32[]{:S(2)}) copy-start(f32[512]{0:T(512)} %param.13) | copy-start | bytes 6148
  28.0 5.0 %copy-start.6 = (bf16[3,512]{1,0:T(4,128)(2,1)S(1)}, bf16[3,512]{1,0:T(4,128)(2,1)}, u32[]{:S(2)}) copy-start(bf16[3,512]{1,0:T(4,128)(2,1)} %param.12) | copy-start | bytes 9220
  30.8 15.1 %copy-start.2 = (bf16[16,4096]{1,0:T(8,128)(2,1)S(1)}, bf16[16,4096]{1,0:T(8,128)(2,1)}, u32[]{:S(2)}) copy-start(bf16[16,4096]{1,0:T(8,128)(2,1)} %get-tuple-element.7.refs_1_) | copy-start | bytes 393220
  30.8 25.1 %collective-permute-start.3 = (bf16[4096,128]{1,0:T(8,128)(2,1)}, bf16[4096,128]{1,0:T(8,128)(2,1)S(1)}, u32[]{:S(2)}, u32[]{:S(2)}) collective-permute-start(bf16[4096,128]{1,0:T(8,128)(2,1)} %get-tuple-element.8.refs_2_), channel_id=1, source_target_pairs={{0,8},{8,0},{1,9},{9,1},{2,10},{10,2},{3,11},{11,3},{4,12},{12,4},... | collective-permute-start | bytes 3145736 | tf_op jit(solution)/shard_map/ppermute | solution.py:270
  33.0 7.2 %collective-permute-start.1 = (bf16[8,512]{1,0:T(8,128)(2,1)S(1)}, bf16[8,512]{1,0:T(8,128)(2,1)S(1)}, u32[]{:S(2)}, u32[]{:S(2)}) collective-permute-start(bf16[8,512]{1,0:T(8,128)(2,1)S(1)} %concatenate.7), channel_id=1, source_target_pairs={{8,0},{16,8},{24,16},{32,24},{40,32},{48,40},{56,48},{64,56},{72,6... | collective-permute-start | bytes 24584 | tf_op jit(solution)/shard_map/ppermute | solution.py:254
  35.0 5.9 %collective-permute-start = (bf16[8,512]{1,0:T(8,128)(2,1)S(1)}, bf16[8,512]{1,0:T(8,128)(2,1)S(1)}, u32[]{:S(2)}, u32[]{:S(2)}) collective-permute-start(bf16[8,512]{1,0:T(8,128)(2,1)S(1)} %concatenate.7), channel_id=1, source_target_pairs={{0,8},{8,16},{16,24},{24,32},{32,40},{40,48},{48,56},{56,64},{64,7... | collective-permute-start | bytes 24584 | tf_op jit(solution)/shard_map/ppermute | solution.py:253
  41.0 4.9 %collective-permute-start.4 = (bf16[8,640]{1,0:T(8,128)(2,1)S(1)}, bf16[8,640]{1,0:T(8,128)(2,1)S(1)}, u32[]{:S(2)}, u32[]{:S(2)}) collective-permute-start(bf16[8,640]{1,0:T(8,128)(2,1)S(1)} %get-tuple-element.10), channel_id=1, source_target_pairs={{0,16},{16,0},{1,17},{17,1},{2,18},{18,2},{3,19},{19,3},{4,20},{20... | collective-permute-start | bytes 30728 | tf_op jit(solution)/shard_map/ppermute | solution.py:261
  45.9 9.9 %collective-permute-start.2 = (bf16[16,4096]{1,0:T(8,128)(2,1)S(1)}, bf16[16,4096]{1,0:T(8,128)(2,1)S(1)}, u32[]{:S(2)}, u32[]{:S(2)}) collective-permute-start(bf16[16,4096]{1,0:T(8,128)(2,1)S(1)} %copy-done.2), channel_id=1, source_target_pairs={{0,8},{8,0},{1,9},{9,1},{2,10},{10,2},{3,11},{11,3},{4,12},{12,4},... | collective-permute-start | bytes 393224 | tf_op jit(solution)/shard_map/ppermute | solution.py:271
  46.9 1.2 %copy-start = (bf16[4096,128]{1,0:T(8,128)(2,1)S(1)}, bf16[4096,128]{1,0:T(8,128)(2,1)}, u32[]{:S(2)}) copy-start(bf16[4096,128]{1,0:T(8,128)(2,1)} %get-tuple-element.8.refs_2_) | copy-start | bytes 3145732
  55.8 11.3 %copy-start.1 = (bf16[4096,128]{1,0:T(8,128)(2,1)S(1)}, bf16[4096,128]{1,0:T(8,128)(2,1)}, u32[]{:S(2)}) copy-start(bf16[4096,128]{1,0:T(8,128)(2,1)} %get-tuple-element.8.refs_2_) | copy-start | bytes 3145732
  63.6 19.0 %collective-permute-start.5 = (f32[528,128]{1,0:T(8,128)S(1)}, f32[528,128]{1,0:T(8,128)S(1)}, u32[]{:S(2)}, u32[]{:S(2)}) collective-permute-start(f32[528,128]{1,0:T(8,128)S(1)} %terms.7), channel_id=1, source_target_pairs={{0,16},{16,0},{1,17},{17,1},{2,18},{18,2},{3,19},{19,3},{4,20},{20... | collective-permute-start | bytes 811016 | tf_op jit(solution)/shard_map/ppermute | solution.py:275
  83.5 5.1 %copy-start.3 = (s32[8]{0:T(128)S(1)}, s32[8]{0:T(128)}, u32[]{:S(2)}) copy-start(s32[8]{0:T(128)} %param.23) | copy-start | bytes 100
  83.5 15.9 %all-to-all-start.1 = ((f32[8,72,128]{2,1,0:T(8,128)}), f32[8,72,128]{2,1,0:T(8,128)S(1)}, u32[]{:S(2)}, u32[]{:S(2)}) async-start(f32[8,72,128]{2,1,0:T(8,128)} %bitcast), calls=%async_computation.1 | async-start | bytes 589824 | tf_op jit(solution)/shard_map/all_to_all | solution.py:282
  100.1 5.3 %copy-start.4 = (f32[8,512]{1,0:T(8,128)S(1)}, f32[8,512]{1,0:T(8,128)}, u32[]{:S(2)}) copy-start(f32[8,512]{1,0:T(8,128)} %param.22) | copy-start | bytes 49156
  100.1 11.9 %all-to-all-start.2 = ((f32[8,72,128]{2,1,0:T(8,128)}), f32[8,72,128]{2,1,0:T(8,128)S(1)}, u32[]{:S(2)}, u32[]{:S(2)}) async-start(f32[8,72,128]{2,1,0:T(8,128)} %broadcast_in_dim.15), calls=%async_computation.2 | async-start | bytes 589824 | tf_op jit(solution)/shard_map/all_to_all | solution.py:285

commit v2 on v1

v2 whole, which is shorter than its diff:
```python
import functools
import math

import jax
import jax.numpy as jnp
import numpy as np
from jax import lax
from jax.experimental import pallas as pl
from jax.experimental.pallas import tpu as pltpu
from jax.sharding import Mesh, PartitionSpec as P

HALO = 8
WAVE = 8.0
SMOOTH = 0.0025
TURN = WAVE / (2.0 * math.pi)
TURN_SQ = TURN * TURN

TGT = ("z", "yh", "core")
SRC = ("yl", "x")


def minimax(func, importance, terms, odd):
    nodes = 0.25 + 0.25 * np.cos(np.linspace(0.0, np.pi, 2001))
    nodes = nodes[nodes > 1e-6]
    scale = nodes if odd else np.ones_like(nodes)
    matter = importance(nodes)
    basis = np.stack([nodes ** (2 * k) for k in range(terms)], 1)
    value = func(nodes) / scale
    weight = np.ones_like(nodes)
    for _ in range(60):
        rows = scale * weight * matter
        coef = np.linalg.lstsq(basis * rows[:, None], value * rows, rcond=None)[0]
        error = np.abs((basis @ coef - value) * scale * matter)
        weight = weight * np.sqrt(1e-12 + error / error.max())
        weight = weight / weight.mean()
    return tuple(float(np.float32(c)) for c in coef)


SIN_POLY = minimax(lambda f: math.sqrt(2.0) * np.sin(np.pi * f), np.ones_like, 3, True)
COS_POLY = minimax(lambda f: math.sqrt(2.0) * np.cos(np.pi * f), lambda f: np.sin(np.pi * f), 3, False)
COS_LEAD = COS_POLY[-1]
COS_MONIC = tuple(c / COS_LEAD for c in COS_POLY[:-1]) + (1.0,)


def horner(z, coef):
    value = z + coef[-2] if coef[-1] == 1.0 else coef[-1] * z + coef[-2]
    for c in coef[-3::-1]:
        value = value * z + c
    return value


def split3(value):
    high = value.astype(jnp.bfloat16).astype(jnp.float32)
    rest = value - high
    mid = rest.astype(jnp.bfloat16).astype(jnp.float32)
    return high, mid, rest - mid


def payload_kernel(factor_ref, points_ref, weight_ref, basis_ref, span_ref, patch_ref, cweight_ref, coef_ref, target_ref, tweight_ref, out_ref, side_ref):
    rounds, controls = cweight_ref.shape
    count = points_ref.shape[2]
    label = lax.broadcasted_iota(jnp.int32, (controls, count), 0)
    pieces = []
    for s in range(rounds):
        span = span_ref[s : s + 1, :]
        patch = patch_ref[s : s + 1, :]
        column = jnp.transpose(jnp.broadcast_to(cweight_ref[s : s + 1, :], (8, controls)))[:, 0:1]
        scaled = []
        for a in range(3):
            picked = jnp.where(label == span + a, column, 0.0)
            scaled.append(basis_ref[a, s : s + 1, :] * jnp.sum(picked, axis=0, keepdims=True))
        denom = scaled[0] + scaled[1] + scaled[2]
        fre = jnp.zeros((1, count), jnp.float32)
        fim = jnp.zeros((1, count), jnp.float32)
        for p in range(factor_ref.shape[2]):
            fre = jnp.where(patch == p, factor_ref[s, 0, p], fre)
            fim = jnp.where(patch == p, factor_ref[s, 1, p], fim)
        weight = weight_ref[s : s + 1, :] / denom
        terms = [value * (weight * fre) for value in scaled] + [value * (weight * fim) for value in scaled]
        high = [t.astype(jnp.bfloat16).astype(jnp.float32) for t in terms]
        low = [t - h for t, h in zip(terms, high)]
        rows = [points_ref[c, s : s + 1, :].astype(jnp.float32) for c in range(3)] + [span.astype(jnp.float32)] + high + low
        pieces.append(jnp.concatenate(rows, axis=0))
    extra = jnp.concatenate(pieces, axis=0).astype(jnp.bfloat16)
    for copy in range(out_ref.shape[0]):
        out_ref[copy, : rounds * controls, :] = coef_ref[...]
        out_ref[copy, rounds * controls :, :] = extra
    parts = [target_ref[...].astype(jnp.float32), *split3(tweight_ref[...])]
    zero = jnp.zeros((2, target_ref.shape[1]), jnp.float32)
    side_ref[...] = jnp.concatenate(parts + [zero], axis=0).astype(jnp.bfloat16)


def source_payload(copies, factor, points, weight, basis, span, patch, cweight, coef, target, tweight):
    rounds, fields, controls = coef.shape
    count = points.shape[2]
    rows = rounds * controls + 16 * rounds
    points = jnp.transpose(points, (1, 0, 2))
    basis = jnp.transpose(basis, (1, 0, 2))
    coef = jnp.transpose(coef, (0, 2, 1)).reshape(rounds * controls, fields)
    vmem = pl.BlockSpec(memory_space=pltpu.VMEM)
    return pl.pallas_call(
        payload_kernel,
        in_specs=[pl.BlockSpec(memory_space=pltpu.SMEM)] + [vmem] * 9,
        out_specs=[vmem, vmem],
        out_shape=[
            jax.ShapeDtypeStruct((copies, rows, count), jnp.bfloat16),
            jax.ShapeDtypeStruct((8, target.shape[1]), jnp.bfloat16),
        ],
        name="payload",
    )(factor, points, weight, basis, span, patch, cweight, coef, target, tweight.reshape(1, -1))


def source_rows(gathered_ref, q, s, rounds, controls):
    first = rounds * controls + 16 * s
    return gathered_ref[q, first : first + 16, :].astype(jnp.float32)


def source_features(gathered_ref, q, rounds, controls):
    pieces = []
    for s in range(rounds):
        pos = source_rows(gathered_ref, q, s, rounds, controls)[0:3]
        norm = pos[0:1] * pos[0:1] + pos[1:2] * pos[1:2] + pos[2:3] * pos[2:3]
        parts = [pos, pos, pos, jnp.ones_like(pos), *split3(norm * TURN_SQ), jnp.zeros_like(norm)]
        pieces.append(jnp.concatenate(parts, axis=0).astype(jnp.bfloat16))
    return jnp.concatenate(pieces, axis=1)


def source_density(gathered_ref, q, rounds, controls):
    count = gathered_ref.shape[2]
    label = lax.broadcasted_iota(jnp.int32, (controls, count), 0).astype(jnp.float32)
    pieces = []
    for s in range(rounds):
        rows = source_rows(gathered_ref, q, s, rounds, controls)
        masks = [label == rows[3:4] + float(a) for a in range(3)]
        spread = []
        for part in range(4):
            value = jnp.zeros((controls, count), jnp.float32)
            for a in range(3):
                value = jnp.where(masks[a], rows[4 + 3 * part + a : 5 + 3 * part + a], value)
            spread.append(value)
        spread = jnp.concatenate(spread, axis=0).astype(jnp.bfloat16)
        plain = gathered_ref[q, s * controls : (s + 1) * controls, :]
        half = plain.shape[1] // 2
        turned = jnp.concatenate([-plain[:, half:], plain[:, :half]], axis=1)
        matrix = jnp.concatenate([plain, turned, plain, turned], axis=0)
        value = lax.dot_general(spread, matrix, (((0,), (0,)), ((), ())), preferred_element_type=jnp.float32)
        pieces.append(value.astype(jnp.bfloat16))
    return jnp.concatenate(pieces, axis=0)


def target_features(target_ref, rows):
    pos = target_ref[...].astype(jnp.float32)
    norm = pos[0:1] * pos[0:1] + pos[1:2] * pos[1:2] + pos[2:3] * pos[2:3] + SMOOTH
    scaled = [*split3(pos[0:3] * (-2.0 * TURN_SQ))]
    ones = jnp.ones((3, pos.shape[1]), jnp.float32)
    side = jnp.concatenate(scaled + [*split3(norm * TURN_SQ), ones, jnp.zeros_like(norm)], axis=0)
    return jnp.transpose(side)[:rows].astype(jnp.bfloat16)


def kernel_terms(square):
    inverse = lax.rsqrt(square)
    turns = square * inverse
    part = turns - jnp.round(turns)
    z = part * part
    sine = part * horner(z, SIN_POLY)
    cosine = horner(z, COS_MONIC)
    scaled = sine * inverse
    kre = (inverse - sine * scaled).astype(jnp.bfloat16)
    kim = (scaled * cosine).astype(jnp.bfloat16)
    return jnp.concatenate([kre, kim], axis=0)


def terms_kernel(make, rounds, controls, has_start, *refs):
    refs = list(refs)
    target_ref = refs.pop(0)
    gathered_ref = refs.pop(0) if make else None
    density_in, feature_in = (None, None) if make else (refs.pop(0), refs.pop(0))
    start_ref = refs.pop(0) if has_start else None
    out_ref = refs.pop(0)
    density_out, feature_out = (refs.pop(0), refs.pop(0)) if make else (None, None)
    side_ref, total_ref = refs
    rows, columns = out_ref.shape
    step = pl.program_id(0)

    @pl.when(step == 0)
    def _():
        side_ref[...] = target_features(target_ref, rows)
        total_ref[...] = jnp.zeros_like(total_ref)

    side = side_ref[...]
    if make:
        chunks, width = gathered_ref.shape[0], rounds * gathered_ref.shape[2]
    else:
        width = 512
        chunks = density_in.shape[0] // width

    def squared(q):
        if make:
            feature = source_features(gathered_ref, q, rounds, controls)
            feature_out[:, q * width : (q + 1) * width] = feature
        else:
            feature = feature_in[:, q * width : (q + 1) * width]
        return jnp.dot(side, feature, preferred_element_type=jnp.float32)

    def densities(q):
        if make:
            density = source_density(gathered_ref, q, rounds, controls)
            density_out[q * width : (q + 1) * width, :] = density
            return density
        return density_in[q * width : (q + 1) * width, :]

    def add(terms, density):
        total_ref[...] += jnp.dot(terms, density, preferred_element_type=jnp.float32)

    square = squared(0)
    ready = None
    for q in range(chunks):
        later = squared(q + 1) if q + 1 < chunks else None
        density = densities(q)
        terms = kernel_terms(square)
        if ready is not None:
            add(*ready)
        ready, square = (terms, density), later
    add(*ready)

    @pl.when(step == pl.num_programs(0) - 1)
    def _():
        plain = total_ref[:rows]
        other = total_ref[rows:] * COS_LEAD
        half = columns // 2
        out = plain + jnp.concatenate([-other[:, half:], other[:, :half]], axis=1)
        if has_start:
            out = out + start_ref[...]
        out_ref[...] = out


def kernel_sums(targets, rows, columns, sources, rounds, controls, start=None):
    make = not isinstance(sources, tuple)
    whole = pl.BlockSpec((rows, columns), lambda i: (0, 0))
    step = 2048
    if make:
        groups, depth, count = sources.shape
        total = groups * rounds * count
        per_step = step // (rounds * count)
        source_specs = [pl.BlockSpec((per_step, depth, count), lambda i: (i, 0, 0))]
        sources = (sources,)
    else:
        total = sources[0].shape[0]
        source_specs = []
    ready_specs = [pl.BlockSpec((step, columns), lambda i: (i, 0)), pl.BlockSpec((16, step), lambda i: (0, i))]
    sums = jax.ShapeDtypeStruct((rows, columns), jnp.float32)
    ready = [
        jax.ShapeDtypeStruct((total, columns), jnp.bfloat16),
        jax.ShapeDtypeStruct((16, total), jnp.bfloat16),
    ]
    in_specs = [pl.BlockSpec(targets.shape, lambda i: (0, 0))] + (source_specs if make else ready_specs)
    args = [targets, *sources]
    if start is not None:
        in_specs.append(whole)
        args.append(start)
    return pl.pallas_call(
        functools.partial(terms_kernel, make, rounds, controls, start is not None),
        grid=(total // step,),
        in_specs=in_specs,
        out_specs=[whole] + ready_specs if make else whole,
        out_shape=[sums] + ready if make else sums,
        scratch_shapes=[pltpu.VMEM((rows, 16), jnp.bfloat16), pltpu.VMEM((2 * rows, columns), jnp.float32)],
        compiler_params=pltpu.CompilerParams(vmem_limit_bytes=24 << 20),
        cost_estimate=pl.CostEstimate(
            flops=rows * total * columns * 8, bytes_accessed=total * columns * 2, transcendentals=rows * total
        ),
        name="terms",
    )(*args)


def band_kernel(scale, offsets_ref, own_ref, side_ref, band_ref, out_ref, pot_ref):
    rows = own_ref.shape[0]
    columns = own_ref.shape[1]
    block = band_ref.shape[1]
    side = side_ref[...].astype(jnp.float32)
    weight = (side[3:4] + side[4:5]) + side[5:6]
    weight = jnp.transpose(jnp.broadcast_to(weight * scale, (8, weight.shape[1])))[:rows, 0:1]
    pot_ref[...] = own_ref[...] * weight
    factors = jnp.transpose(band_ref[...])
    shell = pot_ref[HALO : HALO + block, :]
    for diag in range(band_ref.shape[0]):
        shifted = pot_ref[pl.ds(HALO + offsets_ref[diag], block), :]
        shell = shell + factors[:, diag : diag + 1] * shifted
    shell = shell.astype(jnp.bfloat16)
    for copy in range(out_ref.shape[0]):
        out_ref[copy] = shell


def band_shares(copies, scale, offsets, own, side, band):
    vmem = pl.BlockSpec(memory_space=pltpu.VMEM)
    block, columns = band.shape[1], own.shape[1]
    return pl.pallas_call(
        functools.partial(band_kernel, scale),
        in_specs=[pl.BlockSpec(memory_space=pltpu.SMEM)] + [vmem] * 3,
        out_specs=vmem,
        out_shape=jax.ShapeDtypeStruct((copies, block, columns), jnp.bfloat16),
        scratch_shapes=[pltpu.VMEM(own.shape, jnp.float32)],
        compiler_params=pltpu.CompilerParams(vmem_limit_bytes=16 << 20),
        name="band",
    )(offsets, own, side, band)


def per_device(
    tgt_points, tgt_weight, src_points, src_weight, basis, span, patch, patch_factor, ctrl_weight, ctrl_coef, band, offsets
):
    rows = tgt_points.shape[1]
    rounds, columns, controls = ctrl_coef.shape
    zs = lax.axis_size("z")
    groups = lax.axis_size(SRC)
    blocks = lax.axis_size(TGT)
    swap = [(0, 1), (1, 0)]

    sent, side = source_payload(
        zs, patch_factor, src_points, src_weight, basis, span, patch, ctrl_weight, ctrl_coef, tgt_points, tgt_weight
    )
    partner = lax.ppermute(side, "core", swap)
    links = [(k, k + 1) for k in range(1, blocks - 1, 2)]
    across = lax.ppermute(side, TGT, links + [(b, a) for a, b in links])
    gathered = lax.all_to_all(sent, "z", split_axis=0, concat_axis=0, tiled=True)

    first = lax.axis_index("core") == 0
    span_rows = rows + 2 * HALO
    lanes = -(-span_rows // 128) * 128
    low = jnp.where(first, across, partner)[:, rows - HALO :]
    high = jnp.where(first, partner, across)[:, :HALO]
    wide = jnp.concatenate([low, side, high, jnp.zeros((8, lanes - span_rows), jnp.bfloat16)], axis=1)

    gathered2 = lax.ppermute(gathered, "yh", swap)
    sums, *made = kernel_sums(wide, span_rows, columns, gathered, rounds, controls)
    made = tuple(lax.ppermute(part, "core", swap) for part in made)
    sums, *made2 = kernel_sums(wide, span_rows, columns, gathered2, rounds, controls, sums)
    made2 = tuple(lax.ppermute(part, "core", swap) for part in made2)
    sums = kernel_sums(wide, span_rows, columns, made, rounds, controls, sums)
    sums = kernel_sums(wide, span_rows, columns, made2, rounds, controls, sums)

    source_count = rounds * src_weight.shape[1] * blocks * groups
    scale = TURN / math.sqrt(source_count)
    shares = band_shares(groups, scale, offsets, sums, wide, band)
    shares = lax.all_to_all(shares, SRC, split_axis=0, concat_axis=0, tiled=True)
    return jnp.sum(shares.astype(jnp.float32), axis=0)


def solution(mesh):
    mesh = Mesh(mesh.devices.reshape(8, 2, 2, 2, 4), ("z", "yh", "core", "yl", "x"))
    both = TGT + SRC
    in_specs = (
        P(None, TGT),
        P(TGT),
        P(None, None, both),
        P(None, both),
        P(None, None, both),
        P(None, both),
        P(None, both),
        P(None, None, both),
        P(None, both),
        P(None, None, both),
        P(None, TGT),
        P(),
    )
    return jax.shard_map(
        per_device, mesh=mesh, in_specs=in_specs, out_specs=P(TGT, None), check_vma=False
    )
```

time: 115 us -> 86.3 us (0.75)
  between operations: 10.2 us -> 0.12 us
  starting transfers between devices: 27.9 us -> 20.2 us
  local copies, waits for them, and re-layouts: 7 us -> 0.09 us
  blocking collectives: 22.6 us -> 19.8 us
  waiting for transfers between devices: 8.36 us -> 10.6 us
  Pallas kernels: 35.7 us -> 33.5 us
    ppermute x6 -> x7, starting transfers between devices: 17.5 us -> 11.2 us  [the longest x1 4.72 us: per_device(): across = lax.ppermute(side, TGT, links + [(b, a) for a, b in links])]
    unnamed x19 -> x4, local copies, waits for them, and re-layouts: 4.66 us -> 0.01 us
    all_to_all x1, blocking collectives: 22.6 us -> 19.8 us  [per_device(): lax.all_to_all(shares, SRC, split_axis=0, concat_axis=0, tiled=True)]
    ppermute x6 -> x7, waiting for transfers between devices: 1.74 us -> 4.4 us  [the longest x2 2.24 us: per_device(): made = tuple((lax.ppermute(part, 'core', swap) for part in made))]
    pallas_call x5, Pallas kernels: 33.8 us -> 31.6 us  [the longest x4 30.1 us: kernel_sums(): pl.pallas_call(functools.partial(terms_kernel, make, rounds, controls, st...]
    all_to_all x2 -> x1, starting transfers between devices: 10.4 us -> 9.02 us  [per_device(): lax.all_to_all(sent, 'z', split_axis=0, concat_axis=0, tiled=True)]
    add x2 -> x0, other arithmetic: 1.37 us -> none  [the longest x1 1.33 us: per_device(): shell_field = shell_field + band[diag][:, None] * shifted]
    all_to_all x2 -> x1, waiting for transfers between devices: 6.62 us -> 6.2 us  [per_device(): lax.all_to_all(sent, 'z', split_axis=0, concat_axis=0, tiled=True)]
  transfers between devices with their start and end apart: 8 -> 8, of which waited for: 3 -> 3; matrix products, arithmetic and copies ran while one was open for 1% -> 1% of each run, Pallas kernels for 20% -> 27%
where the time goes in v2:
time: 86.3 us; the launch traced here: 86 us
  Pallas kernels  33.5 us (39%)
  starting transfers between devices  20.2 us (23%)
  blocking collectives  19.8 us (23%)
  waiting for transfers between devices  10.6 us (12%)
  other arithmetic  1.7 us (2%)
    pallas_call x4, Pallas kernels, kernel_sums(): pl.pallas_call(functools.partial(terms_kernel, make, rounds, controls, st...  30.1 us
    all_to_all x1, blocking collectives, per_device(): lax.all_to_all(shares, SRC, split_axis=0, concat_axis=0, tiled=True)  19.8 us
    all_to_all x1, starting transfers between devices, per_device(): lax.all_to_all(sent, 'z', split_axis=0, concat_axis=0, tiled=True)  9.02 us
    all_to_all x1, waiting for transfers between devices, per_device(): lax.all_to_all(sent, 'z', split_axis=0, concat_axis=0, tiled=True)  6.2 us
    ppermute x1, starting transfers between devices, per_device(): across = lax.ppermute(side, TGT, links + [(b, a) for a, b in links])  4.72 us
    ppermute x1, starting transfers between devices, per_device(): gathered2 = lax.ppermute(gathered, 'yh', swap)  2.91 us
    ppermute x2, starting transfers between devices, per_device(): made = tuple((lax.ppermute(part, 'core', swap) for part in made))  2.36 us
    ppermute x2, waiting for transfers between devices, per_device(): made = tuple((lax.ppermute(part, 'core', swap) for part in made))  2.24 us
  transfers between devices with their start and end apart: 8, of which 3 were waited for; matrix products, arithmetic and copies ran while one was open for 1% of the time, Pallas kernels for 27%

profile of v2, /device:TPU:1, one launch (start us, length us, event | category | flops | bytes accessed | tf_op | source)
XLA Modules:
  0.0 86.0 jit_solution(13960050945945187233)
XLA Ops:
  0.0 1.8 %payload.1 = (bf16[8,192,128]{2,1,0:T(8,128)(2,1)}, bf16[8,512]{1,0:T(8,128)(2,1)}) custom-call(f32[4,2,4]{2,1,0:T(2,128)} %factor_ref.1, bf16[3,4,128]{2,1,0:T(4,128)(2,1)} %bitcast.8, f32[4,128]{1,0:T(4,128)} %weight_ref.1, f32[3,4,128]{2,1,0:T(4,128)} %bitcast.7, s32[4,128]{1,0:T(4,128)} %span_ref.1, s32[4,128]{1,0:T(4,128)} %patch_ref.1, ...), custom_call_target="tpu_custom_call" | custom-call | tf_op jit(solution)/shard_map/payload/pallas_call | solution.py:101
  1.8 9.0 %all-to-all-start = ((bf16[8,192,128]{2,1,0:T(8,128)(2,1)}), bf16[8,192,128]{2,1,0:T(8,128)(2,1)S(1)}, u32[]{:S(2)}, u32[]{:S(2)}) async-start(bf16[8,192,128]{2,1,0:T(8,128)(2,1)} %get-tuple-element.14), calls=%async_computation | async-start | bytes 786432 | tf_op jit(solution)/shard_map/all_to_all | solution.py:324
  10.9 1.0 %collective-permute-start.1 = (bf16[8,512]{1,0:T(8,128)(2,1)}, bf16[8,512]{1,0:T(8,128)(2,1)S(1)}, u32[]{:S(2)}, u32[]{:S(2)}) collective-permute-start(bf16[8,512]{1,0:T(8,128)(2,1)} %get-tuple-element.13), channel_id=1, source_target_pairs={{0,8},{8,0},{1,9},{9,1},{2,10},{10,2},{3,11},{11,3},{4,12},{12,4},... | collective-permute-start | bytes 24584 | tf_op jit(solution)/shard_map/ppermute | solution.py:321
  11.8 4.7 %collective-permute-start = (bf16[8,512]{1,0:T(8,128)(2,1)}, bf16[8,512]{1,0:T(8,128)(2,1)S(1)}, u32[]{:S(2)}, u32[]{:S(2)}) collective-permute-start(bf16[8,512]{1,0:T(8,128)(2,1)} %get-tuple-element.13), channel_id=1, source_target_pairs={{8,16},{24,32},{40,48},{56,64},{72,80},{88,96},{104,112},{120,128}... | collective-permute-start | bytes 24584 | tf_op jit(solution)/shard_map/ppermute | solution.py:323
  16.6 0.1 pad.3.clone
  16.6 2.1 %collective-permute-done = bf16[8,512]{1,0:T(8,128)(2,1)S(1)} collective-permute-done((bf16[8,512]{1,0:T(8,128)(2,1)}, bf16[8,512]{1,0:T(8,128)(2,1)S(1)}, u32[]{:S(2)}, u32[]{:S(2)}) %collective-permute-start) | collective-permute-done | bytes 8224 | tf_op jit(solution)/shard_map/ppermute | solution.py:323
  18.8 0.1 slice_select_fusion.1
  18.9 6.2 %all-to-all-done.refs_1_ = bf16[8,192,128]{2,1,0:T(8,128)(2,1)S(1)} async-done(((bf16[8,192,128]{2,1,0:T(8,128)(2,1)}), bf16[8,192,128]{2,1,0:T(8,128)(2,1)S(1)}, u32[]{:S(2)}, u32[]{:S(2)}) %all-to-all-start) | async-done | bytes 393248 | tf_op jit(solution)/shard_map/all_to_all | solution.py:324
  25.1 2.9 %collective-permute-start.2 = (bf16[8,192,128]{2,1,0:T(8,128)(2,1)S(1)}, bf16[8,192,128]{2,1,0:T(8,128)(2,1)S(1)}, u32[]{:S(2)}, u32[]{:S(2)}) collective-permute-start(bf16[8,192,128]{2,1,0:T(8,128)(2,1)S(1)} %all-to-all-done.refs_1_), channel_id=1, source_target_pairs={{0,16},{16,0},{1,17},{17,1},{2,18},{18,2},{3,19},{19,3},{4,20},{20... | collective-permute-start | bytes 1179656 | tf_op jit(solution)/shard_map/ppermute | solution.py:333
  28.0 0.8 maximum_maximum_fusion.refs_0_.side_ref
  28.7 8.4 %terms.4 = (f32[528,128]{1,0:T(8,128)S(1)}, bf16[4096,128]{1,0:T(8,128)(2,1)S(1)}, bf16[16,4096]{1,0:T(8,128)(2,1)S(1)}) custom-call(bf16[8,640]{1,0:T(8,128)(2,1)S(1)} %maximum_maximum_fusion.refs_0_.side_ref, bf16[8,192,128]{2,1,0:T(8,128)(2,1)S(1)} %all-to-all-done.refs_1_), custom_call_target="tpu_custom_call" | custom-call | flops 2214592512 | bytes 1048576 | tf_op jit(solution)/shard_map/terms/pallas_call | solution.py:261
  37.1 1.9 %collective-permute-start.5 = (bf16[4096,128]{1,0:T(8,128)(2,1)S(1)}, bf16[4096,128]{1,0:T(8,128)(2,1)S(1)}, u32[]{:S(2)}, u32[]{:S(2)}) collective-permute-start(bf16[4096,128]{1,0:T(8,128)(2,1)S(1)} %get-tuple-element.18), channel_id=1, source_target_pairs={{0,8},{8,0},{1,9},{9,1},{2,10},{10,2},{3,11},{11,3},{4,12},{12,4},... | collective-permute-start | bytes 3145736 | tf_op jit(solution)/shard_map/ppermute | solution.py:335
  39.0 8.3 %terms.5 = (f32[528,128]{1,0:T(8,128)S(1)}, bf16[4096,128]{1,0:T(8,128)(2,1)S(1)}, bf16[16,4096]{1,0:T(8,128)(2,1)S(1)}) custom-call(bf16[8,640]{1,0:T(8,128)(2,1)S(1)} %maximum_maximum_fusion.refs_0_.side_ref, bf16[8,192,128]{2,1,0:T(8,128)(2,1)S(1)} %collective-permute-done.2.refs_1_, f32[528,128]{1,0:T(8,128)S(1)} %get-tuple-element.15.refs_2_), custom_call_target="tpu_custom_call" | custom-call | flops 2214592512 | bytes 1048576 | tf_op jit(solution)/shard_map/terms/pallas_call | solution.py:261
  47.4 0.1 collective-permute-start.3
  47.5 0.5 collective-permute-start.6
  48.0 0.1 collective-permute-start.4
  48.1 2.2 %collective-permute-done.6.refs_2_ = bf16[16,4096]{1,0:T(8,128)(2,1)S(1)} collective-permute-done((bf16[16,4096]{1,0:T(8,128)(2,1)S(1)}, bf16[16,4096]{1,0:T(8,128)(2,1)S(1)}, u32[]{:S(2)}, u32[]{:S(2)}) %collective-permute-start.6) | collective-permute-done | bytes 131104 | tf_op jit(solution)/shard_map/ppermute | solution.py:335
  50.3 6.7 %terms.6.refs_3_ = f32[528,128]{1,0:T(8,128)S(1)} custom-call(bf16[8,640]{1,0:T(8,128)(2,1)S(1)} %maximum_maximum_fusion.refs_0_.side_ref, bf16[4096,128]{1,0:T(8,128)(2,1)S(1)} %collective-permute-done.5.refs_1_, bf16[16,4096]{1,0:T(8,128)(2,1)S(1)} %collective-permute-done.6.refs_2_, f32[528,128]{1,0:T(8,128)S(1)} %get-tuple-element.20.refs_3_), custom_call_target="tpu_custom_call" | custom-call | flops 2214592512 | bytes 1048576 | tf_op jit(solution)/shard_map/terms/pallas_call | solution.py:261
  57.0 0.0 copy-start
  57.0 0.0 copy-start.1
  57.0 6.7 %terms.7.own_ref = f32[528,128]{1,0:T(8,128)S(1)} custom-call(bf16[8,640]{1,0:T(8,128)(2,1)S(1)} %maximum_maximum_fusion.refs_0_.side_ref, bf16[4096,128]{1,0:T(8,128)(2,1)S(1)} %collective-permute-done.3.refs_1_, bf16[16,4096]{1,0:T(8,128)(2,1)S(1)} %collective-permute-done.4.refs_2_, f32[528,128]{1,0:T(8,128)S(1)} %terms.6.refs_3_), custom_call_target="tpu_custom_call" | custom-call | flops 2214592512 | bytes 1048576 | tf_op jit(solution)/shard_map/terms/pallas_call | solution.py:261
  63.8 1.5 %band.1 = bf16[8,512,128]{2,1,0:T(8,128)(2,1)S(1)} custom-call(s32[8]{0:T(128)S(1)} %copy-done.1, f32[528,128]{1,0:T(8,128)S(1)} %terms.7.own_ref, bf16[8,640]{1,0:T(8,128)(2,1)S(1)} %maximum_maximum_fusion.refs_0_.side_ref, f32[8,512]{1,0:T(8,128)S(1)} %copy-done), custom_call_target="tpu_custom_call" | custom-call | tf_op jit(solution)/shard_map/band/pallas_call | solution.py:297
  65.3 19.8 %all_to_all.10 = bf16[8,512,128]{2,1,0:T(8,128)(2,1)S(1)} all-to-all(bf16[8,512,128]{2,1,0:T(8,128)(2,1)S(1)} %band.1), channel_id=1, replica_groups=mesh['z'=8,'yh'=2,'core'=2,'yl'=2,'x'=4] {'yl','x'}, dimensions={0} | all-to-all | bytes 2097152 | tf_op jit(solution)/shard_map/all_to_all | solution.py:344
  85.1 0.8 convert_reduce_fusion
  (8 shorter events, 0.0 us)
Async XLA Ops:
  1.8 23.2 %all-to-all-start = ((bf16[8,192,128]{2,1,0:T(8,128)(2,1)}), bf16[8,192,128]{2,1,0:T(8,128)(2,1)S(1)}, u32[]{:S(2)}, u32[]{:S(2)}) async-start(bf16[8,192,128]{2,1,0:T(8,128)(2,1)} %get-tuple-element.14), calls=%async_computation | async-start | bytes 786432 | tf_op jit(solution)/shard_map/all_to_all | solution.py:324
  10.9 5.8 %collective-permute-start.1 = (bf16[8,512]{1,0:T(8,128)(2,1)}, bf16[8,512]{1,0:T(8,128)(2,1)S(1)}, u32[]{:S(2)}, u32[]{:S(2)}) collective-permute-start(bf16[8,512]{1,0:T(8,128)(2,1)} %get-tuple-element.13), channel_id=1, source_target_pairs={{0,8},{8,0},{1,9},{9,1},{2,10},{10,2},{3,11},{11,3},{4,12},{12,4},... | collective-permute-start | bytes 24584 | tf_op jit(solution)/shard_map/ppermute | solution.py:321
  11.8 7.0 %collective-permute-start = (bf16[8,512]{1,0:T(8,128)(2,1)}, bf16[8,512]{1,0:T(8,128)(2,1)S(1)}, u32[]{:S(2)}, u32[]{:S(2)}) collective-permute-start(bf16[8,512]{1,0:T(8,128)(2,1)} %get-tuple-element.13), channel_id=1, source_target_pairs={{8,16},{24,32},{40,48},{56,64},{72,80},{88,96},{104,112},{120,128}... | collective-permute-start | bytes 24584 | tf_op jit(solution)/shard_map/ppermute | solution.py:323
  25.1 13.9 %collective-permute-start.2 = (bf16[8,192,128]{2,1,0:T(8,128)(2,1)S(1)}, bf16[8,192,128]{2,1,0:T(8,128)(2,1)S(1)}, u32[]{:S(2)}, u32[]{:S(2)}) collective-permute-start(bf16[8,192,128]{2,1,0:T(8,128)(2,1)S(1)} %all-to-all-done.refs_1_), channel_id=1, source_target_pairs={{0,16},{16,0},{1,17},{17,1},{2,18},{18,2},{3,19},{19,3},{4,20},{20... | collective-permute-start | bytes 1179656 | tf_op jit(solution)/shard_map/ppermute | solution.py:333
  37.1 13.2 %collective-permute-start.5 = (bf16[4096,128]{1,0:T(8,128)(2,1)S(1)}, bf16[4096,128]{1,0:T(8,128)(2,1)S(1)}, u32[]{:S(2)}, u32[]{:S(2)}) collective-permute-start(bf16[4096,128]{1,0:T(8,128)(2,1)S(1)} %get-tuple-element.18), channel_id=1, source_target_pairs={{0,8},{8,0},{1,9},{9,1},{2,10},{10,2},{3,11},{11,3},{4,12},{12,4},... | collective-permute-start | bytes 3145736 | tf_op jit(solution)/shard_map/ppermute | solution.py:335
  47.4 9.7 %collective-permute-start.3 = (bf16[4096,128]{1,0:T(8,128)(2,1)S(1)}, bf16[4096,128]{1,0:T(8,128)(2,1)S(1)}, u32[]{:S(2)}, u32[]{:S(2)}) collective-permute-start(bf16[4096,128]{1,0:T(8,128)(2,1)S(1)} %get-tuple-element.16), channel_id=1, source_target_pairs={{0,8},{8,0},{1,9},{9,1},{2,10},{10,2},{3,11},{11,3},{4,12},{12,4},... | collective-permute-start | bytes 3145736 | tf_op jit(solution)/shard_map/ppermute | solution.py:337
  47.5 2.8 %collective-permute-start.6 = (bf16[16,4096]{1,0:T(8,128)(2,1)S(1)}, bf16[16,4096]{1,0:T(8,128)(2,1)S(1)}, u32[]{:S(2)}, u32[]{:S(2)}) collective-permute-start(bf16[16,4096]{1,0:T(8,128)(2,1)S(1)} %get-tuple-element.19), channel_id=1, source_target_pairs={{0,8},{8,0},{1,9},{9,1},{2,10},{10,2},{3,11},{11,3},{4,12},{12,4},... | collective-permute-start | bytes 393224 | tf_op jit(solution)/shard_map/ppermute | solution.py:335
  48.0 9.1 %collective-permute-start.4 = (bf16[16,4096]{1,0:T(8,128)(2,1)S(1)}, bf16[16,4096]{1,0:T(8,128)(2,1)S(1)}, u32[]{:S(2)}, u32[]{:S(2)}) collective-permute-start(bf16[16,4096]{1,0:T(8,128)(2,1)S(1)} %get-tuple-element.17), channel_id=1, source_target_pairs={{0,8},{8,0},{1,9},{9,1},{2,10},{10,2},{3,11},{11,3},{4,12},{12,4},... | collective-permute-start | bytes 393224 | tf_op jit(solution)/shard_map/ppermute | solution.py:337
  57.0 6.8 %copy-start = (f32[8,512]{1,0:T(8,128)S(1)}, f32[8,512]{1,0:T(8,128)}, u32[]{:S(2)}) copy-start(f32[8,512]{1,0:T(8,128)} %band_ref.1) | copy-start | bytes 49156
  57.0 6.8 %copy-start.1 = (s32[8]{0:T(128)S(1)}, s32[8]{0:T(128)}, u32[]{:S(2)}) copy-start(s32[8]{0:T(128)} %offsets_ref.1) | copy-start | bytes 100

commit v3 on v2

--- a/solution.py
+++ b/solution.py
@@ -122,7 +122,7 @@
         norm = pos[0:1] * pos[0:1] + pos[1:2] * pos[1:2] + pos[2:3] * pos[2:3]
         parts = [pos, pos, pos, jnp.ones_like(pos), *split3(norm * TURN_SQ), jnp.zeros_like(norm)]
         pieces.append(jnp.concatenate(parts, axis=0).astype(jnp.bfloat16))
-    return jnp.concatenate(pieces, axis=1)
+    return pieces
 
 
 def source_density(gathered_ref, q, rounds, controls):
@@ -148,8 +148,20 @@
     return jnp.concatenate(pieces, axis=0)
 
 
-def target_features(target_ref, rows):
-    pos = target_ref[...].astype(jnp.float32)
+def widened(low, middle, high, rows, lanes):
+    count = middle.shape[1]
+    place = lax.broadcasted_iota(jnp.int32, (8, lanes), 1)
+
+    def moved(value, shift):
+        pad = jnp.concatenate([value, jnp.zeros((8, lanes - count), jnp.float32)], axis=1)
+        return pltpu.roll(pad, shift % lanes, 1)
+
+    inner = jnp.where(place < HALO + count, moved(middle, HALO), moved(high, HALO + count))
+    outer = jnp.where(place < HALO, moved(low, HALO - count), inner)
+    return jnp.where(place < rows, outer, 0.0)
+
+
+def target_features(pos, rows):
     norm = pos[0:1] * pos[0:1] + pos[1:2] * pos[1:2] + pos[2:3] * pos[2:3] + SMOOTH
     scaled = [*split3(pos[0:3] * (-2.0 * TURN_SQ))]
     ones = jnp.ones((3, pos.shape[1]), jnp.float32)
@@ -170,117 +182,146 @@
     return jnp.concatenate([kre, kim], axis=0)
 
 
-def terms_kernel(make, rounds, controls, has_start, *refs):
+def terms_kernel(first, make, rounds, controls, *refs):
     refs = list(refs)
-    target_ref = refs.pop(0)
-    gathered_ref = refs.pop(0) if make else None
-    density_in, feature_in = (None, None) if make else (refs.pop(0), refs.pop(0))
-    start_ref = refs.pop(0) if has_start else None
-    out_ref = refs.pop(0)
-    density_out, feature_out = (refs.pop(0), refs.pop(0)) if make else (None, None)
-    side_ref, total_ref = refs
-    rows, columns = out_ref.shape
+    if first:
+        core_ref, block_ref, other_ref, source_ref, out_ref, wide_ref, side_ref, total_ref = refs
+        ready_ref = None
+    elif make:
+        wide_ref, source_ref, start_ref, out_ref, ready_ref, side_ref, total_ref = refs
+    else:
+        wide_ref, source_ref, start_ref, out_ref, side_ref, total_ref = refs
+        ready_ref = source_ref
+    tiles, rows, columns = out_ref.shape
+    count = source_ref.shape[-1]
+    width = rounds * count
+    depth = width + 16 * rounds
+    chunks = source_ref.shape[0] if make else source_ref.shape[0] // depth
     step = pl.program_id(0)
 
     @pl.when(step == 0)
     def _():
-        side_ref[...] = target_features(target_ref, rows)
+        if first:
+            lanes = wide_ref.shape[2]
+            low_core = core_ref[0] == 0
+            block, across = block_ref[:8].astype(jnp.float32), block_ref[8:].astype(jnp.float32)
+            other, beyond = other_ref[:8].astype(jnp.float32), other_ref[8:].astype(jnp.float32)
+            pick = lambda a, b: jnp.where(low_core, a, b)
+            wide_ref[0] = widened(pick(across, other), block, pick(other, across), rows, lanes)
+            wide_ref[1] = widened(pick(block, beyond), other, pick(beyond, block), rows, lanes)
+        for t in range(tiles):
+            side_ref[t] = target_features(wide_ref[t], rows)
         total_ref[...] = jnp.zeros_like(total_ref)
 
-    side = side_ref[...]
-    if make:
-        chunks, width = gathered_ref.shape[0], rounds * gathered_ref.shape[2]
-    else:
-        width = 512
-        chunks = density_in.shape[0] // width
-
-    def squared(q):
-        if make:
-            feature = source_features(gathered_ref, q, rounds, controls)
-            feature_out[:, q * width : (q + 1) * width] = feature
-        else:
-            feature = feature_in[:, q * width : (q + 1) * width]
-        return jnp.dot(side, feature, preferred_element_type=jnp.float32)
-
-    def densities(q):
-        if make:
-            density = source_density(gathered_ref, q, rounds, controls)
-            density_out[q * width : (q + 1) * width, :] = density
-            return density
-        return density_in[q * width : (q + 1) * width, :]
-
-    def add(terms, density):
-        total_ref[...] += jnp.dot(terms, density, preferred_element_type=jnp.float32)
-
-    square = squared(0)
-    ready = None
-    for q in range(chunks):
-        later = squared(q + 1) if q + 1 < chunks else None
-        density = densities(q)
+    features, densities = {}, {}
+
+    def squared(q, t):
+        if q not in features:
+            places = [slice(q * depth + width + 16 * s, q * depth + width + 16 * (s + 1)) for s in range(rounds)]
+            if make:
+                pieces = source_features(source_ref, q, rounds, controls)
+                if ready_ref is not None:
+                    for place, piece in zip(places, pieces):
+                        ready_ref[place, :] = piece
+            else:
+                pieces = [ready_ref[place, :] for place in places]
+            features[q] = jnp.concatenate(pieces, axis=1)
+        return jnp.dot(side_ref[t], features[q], preferred_element_type=jnp.float32)
+
+    def density(q):
+        if q not in densities:
+            place = slice(q * depth, q * depth + width)
+            if make:
+                densities[q] = source_density(source_ref, q, rounds, controls)
+                if ready_ref is not None:
+                    ready_ref[place, :] = densities[q]
+            else:
+                densities[q] = ready_ref[place, :]
+        return densities[q]
+
+    def add(terms, q, t):
+        total_ref[t] += jnp.dot(terms, density(q), preferred_element_type=jnp.float32)
+
+    items = [(q, t) for q in range(chunks) for t in range(tiles)]
+    square = squared(*items[0])
+    waiting = None
+    for n, (q, t) in enumerate(items):
+        later = squared(*items[n + 1]) if n + 1 < len(items) else None
+        density(q)
         terms = kernel_terms(square)
-        if ready is not None:
-            add(*ready)
-        ready, square = (terms, density), later
-    add(*ready)
+        if waiting is not None:
+            add(*waiting)
+        waiting, square = (terms, q, t), later
+    add(*waiting)
 
     @pl.when(step == pl.num_programs(0) - 1)
     def _():
-        plain = total_ref[:rows]
-        other = total_ref[rows:] * COS_LEAD
-        half = columns // 2
-        out = plain + jnp.concatenate([-other[:, half:], other[:, :half]], axis=1)
-        if has_start:
-            out = out + start_ref[...]
-        out_ref[...] = out
-
-
-def kernel_sums(targets, rows, columns, sources, rounds, controls, start=None):
-    make = not isinstance(sources, tuple)
-    whole = pl.BlockSpec((rows, columns), lambda i: (0, 0))
-    step = 2048
+        for t in range(tiles):
+            plain = total_ref[t, :rows]
+            other = total_ref[t, rows:] * COS_LEAD
+            half = columns // 2
+            out = plain + jnp.concatenate([-other[:, half:], other[:, :half]], axis=1)
+            if not first:
+                out = out + start_ref[t]
+            out_ref[t] = out
+
+
+def kernel_sums(rows, lanes, sources, rounds, controls, make, blocks=None, wide=None, start=None, tile=0):
+    first = blocks is not None
+    tiles = 2 if first else 1
+    count = sources.shape[-1]
+    chunk = rounds * count + 16 * rounds
+    per_step = 2 if first else 4
     if make:
-        groups, depth, count = sources.shape
-        total = groups * rounds * count
-        per_step = step // (rounds * count)
-        source_specs = [pl.BlockSpec((per_step, depth, count), lambda i: (i, 0, 0))]
-        sources = (sources,)
+        chunks = sources.shape[0]
+        source_spec = pl.BlockSpec((per_step,) + sources.shape[1:], lambda i: (i, 0, 0))
     else:
-        total = sources[0].shape[0]
-        source_specs = []
-    ready_specs = [pl.BlockSpec((step, columns), lambda i: (i, 0)), pl.BlockSpec((16, step), lambda i: (0, i))]
-    sums = jax.ShapeDtypeStruct((rows, columns), jnp.float32)
-    ready = [
-        jax.ShapeDtypeStruct((total, columns), jnp.bfloat16),
-        jax.ShapeDtypeStruct((16, total), jnp.bfloat16),
-    ]
-    in_specs = [pl.BlockSpec(targets.shape, lambda i: (0, 0))] + (source_specs if make else ready_specs)
-    args = [targets, *sources]
-    if start is not None:
-        in_specs.append(whole)
-        args.append(start)
+        chunks = sources.shape[0] // chunk
+        source_spec = pl.BlockSpec((per_step * chunk, count), lambda i: (i, 0))
+    out_specs = [pl.BlockSpec((tiles, rows, count), lambda i: (0, 0, 0))]
+    out_shape = [jax.ShapeDtypeStruct((tiles, rows, count), jnp.float32)]
+    if first:
+        core, block, other = blocks
+        whole = pl.BlockSpec(block.shape, lambda i: (0, 0))
+        in_specs = [pl.BlockSpec(memory_space=pltpu.SMEM), whole, whole, source_spec]
+        args = [core, block, other, sources]
+        out_specs.append(pl.BlockSpec((2, 8, lanes), lambda i: (0, 0, 0)))
+        out_shape.append(jax.ShapeDtypeStruct((2, 8, lanes), jnp.float32))
+    else:
+        in_specs = [
+            pl.BlockSpec((1, 8, lanes), lambda i: (tile, 0, 0)),
+            source_spec,
+            pl.BlockSpec((1, rows, count), lambda i: (tile, 0, 0)),
+        ]
+        args = [wide, sources, start]
+        if make:
+            out_specs.append(pl.BlockSpec((per_step * chunk, count), lambda i: (i, 0)))
+            out_shape.append(jax.ShapeDtypeStruct((chunks * chunk, count), jnp.bfloat16))
+    pairs = tiles * rows * chunks * rounds * count
     return pl.pallas_call(
-        functools.partial(terms_kernel, make, rounds, controls, start is not None),
-        grid=(total // step,),
+        functools.partial(terms_kernel, first, make, rounds, controls),
+        grid=(chunks // per_step,),
         in_specs=in_specs,
-        out_specs=[whole] + ready_specs if make else whole,
-        out_shape=[sums] + ready if make else sums,
-        scratch_shapes=[pltpu.VMEM((rows, 16), jnp.bfloat16), pltpu.VMEM((2 * rows, columns), jnp.float32)],
+        out_specs=out_specs,
+        out_shape=out_shape,
+        scratch_shapes=[
+            pltpu.VMEM((tiles, rows, 16), jnp.bfloat16),
+            pltpu.VMEM((tiles, 2 * rows, count), jnp.float32),
+        ],
         compiler_params=pltpu.CompilerParams(vmem_limit_bytes=24 << 20),
-        cost_estimate=pl.CostEstimate(
-            flops=rows * total * columns * 8, bytes_accessed=total * columns * 2, transcendentals=rows * total
-        ),
+        cost_estimate=pl.CostEstimate(flops=pairs * count * 8, bytes_accessed=1 << 20, transcendentals=pairs),
         name="terms",
     )(*args)
 
 
-def band_kernel(scale, offsets_ref, own_ref, side_ref, band_ref, out_ref, pot_ref):
+def band_kernel(scale, offsets_ref, own_ref, arrived_ref, side_ref, band_ref, out_ref, pot_ref):
     rows = own_ref.shape[0]
     columns = own_ref.shape[1]
     block = band_ref.shape[1]
-    side = side_ref[...].astype(jnp.float32)
+    side = side_ref[...]
     weight = (side[3:4] + side[4:5]) + side[5:6]
     weight = jnp.transpose(jnp.broadcast_to(weight * scale, (8, weight.shape[1])))[:rows, 0:1]
-    pot_ref[...] = own_ref[...] * weight
+    pot_ref[...] = (own_ref[...] + arrived_ref[...]) * weight
     factors = jnp.transpose(band_ref[...])
     shell = pot_ref[HALO : HALO + block, :]
     for diag in range(band_ref.shape[0]):
@@ -291,18 +332,18 @@
         out_ref[copy] = shell
 
 
-def band_shares(copies, scale, offsets, own, side, band):
+def band_shares(copies, scale, offsets, own, arrived, side, band):
     vmem = pl.BlockSpec(memory_space=pltpu.VMEM)
     block, columns = band.shape[1], own.shape[1]
     return pl.pallas_call(
         functools.partial(band_kernel, scale),
-        in_specs=[pl.BlockSpec(memory_space=pltpu.SMEM)] + [vmem] * 3,
+        in_specs=[pl.BlockSpec(memory_space=pltpu.SMEM)] + [vmem] * 4,
         out_specs=vmem,
         out_shape=jax.ShapeDtypeStruct((copies, block, columns), jnp.bfloat16),
         scratch_shapes=[pltpu.VMEM(own.shape, jnp.float32)],
         compiler_params=pltpu.CompilerParams(vmem_limit_bytes=16 << 20),
         name="band",
-    )(offsets, own, side, band)
+    )(offsets, own, arrived, side, band)
 
 
 def per_device(
@@ -318,29 +359,25 @@
     sent, side = source_payload(
         zs, patch_factor, src_points, src_weight, basis, span, patch, ctrl_weight, ctrl_coef, tgt_points, tgt_weight
     )
-    partner = lax.ppermute(side, "core", swap)
     links = [(k, k + 1) for k in range(1, blocks - 1, 2)]
     across = lax.ppermute(side, TGT, links + [(b, a) for a, b in links])
     gathered = lax.all_to_all(sent, "z", split_axis=0, concat_axis=0, tiled=True)
-
-    first = lax.axis_index("core") == 0
+    block = jnp.concatenate([side, across], axis=0)
+    other = lax.ppermute(block, "core", swap)
+    core = lax.axis_index("core").astype(jnp.int32).reshape(1)
+
     span_rows = rows + 2 * HALO
     lanes = -(-span_rows // 128) * 128
-    low = jnp.where(first, across, partner)[:, rows - HALO :]
-    high = jnp.where(first, partner, across)[:, :HALO]
-    wide = jnp.concatenate([low, side, high, jnp.zeros((8, lanes - span_rows), jnp.bfloat16)], axis=1)
-
     gathered2 = lax.ppermute(gathered, "yh", swap)
-    sums, *made = kernel_sums(wide, span_rows, columns, gathered, rounds, controls)
-    made = tuple(lax.ppermute(part, "core", swap) for part in made)
-    sums, *made2 = kernel_sums(wide, span_rows, columns, gathered2, rounds, controls, sums)
-    made2 = tuple(lax.ppermute(part, "core", swap) for part in made2)
-    sums = kernel_sums(wide, span_rows, columns, made, rounds, controls, sums)
-    sums = kernel_sums(wide, span_rows, columns, made2, rounds, controls, sums)
+    shapes = (span_rows, lanes)
+    sums, wide = kernel_sums(*shapes, gathered, rounds, controls, True, blocks=(core, block, other))
+    share, made = kernel_sums(*shapes, gathered2, rounds, controls, True, wide=wide, start=sums, tile=1)
+    arrived = lax.ppermute(share, "core", swap)
+    (own,) = kernel_sums(*shapes, made, rounds, controls, False, wide=wide, start=sums, tile=0)
 
     source_count = rounds * src_weight.shape[1] * blocks * groups
     scale = TURN / math.sqrt(source_count)
-    shares = band_shares(groups, scale, offsets, sums, wide, band)
+    shares = band_shares(groups, scale, offsets, own[0], arrived[0], wide[0], band)
     shares = lax.all_to_all(shares, SRC, split_axis=0, concat_axis=0, tiled=True)
     return jnp.sum(shares.astype(jnp.float32), axis=0)
 

time: 86.3 us -> 81.5 us (0.944)
  waiting for transfers between devices: 10.6 us -> 7.83 us
  Pallas kernels: 33.5 us -> 32.2 us
    ppermute x5 -> x2, waiting for transfers between devices: 2.25 us -> 0.01 us  [the longest x1 0.01 us: per_device(): other = lax.ppermute(block, 'core', swap)]
    ppermute x5 -> x2, starting transfers between devices: 3.55 us -> 2.08 us  [the longest x1 2.08 us: per_device(): arrived = lax.ppermute(share, 'core', swap)]
    pallas_call x4 -> x3, Pallas kernels: 30.1 us -> 28.9 us  [kernel_sums(): pl.pallas_call(functools.partial(terms_kernel, first, make, rounds, contr...]
    ppermute x1, waiting for transfers between devices: 2.15 us -> 1.12 us  [per_device(): across = lax.ppermute(side, TGT, links + [(b, a) for a, b in links])]
    ppermute x1, starting transfers between devices: 4.72 us -> 5.65 us  [per_device(): across = lax.ppermute(side, TGT, links + [(b, a) for a, b in links])]
  transfers between devices with their start and end apart: 8 -> 5, of which waited for: 3 -> 2; matrix products, arithmetic and copies ran while one was open for 1% -> 1% of each run, Pallas kernels for 27% -> 25%
where the time goes in v3:
time: 81.5 us; the launch traced here: 81.2 us
  Pallas kernels  32.2 us (40%)
  blocking collectives  19.8 us (24%)
  starting transfers between devices  19.7 us (24%)
  waiting for transfers between devices  7.83 us (10%)
  other arithmetic  0.85 us (1%)
    pallas_call x3, Pallas kernels, kernel_sums(): pl.pallas_call(functools.partial(terms_kernel, first, make, rounds, contr...  28.9 us
    all_to_all x1, blocking collectives, per_device(): lax.all_to_all(shares, SRC, split_axis=0, concat_axis=0, tiled=True)  19.8 us
    all_to_all x1, starting transfers between devices, per_device(): lax.all_to_all(sent, 'z', split_axis=0, concat_axis=0, tiled=True)  9.02 us
    all_to_all x1, waiting for transfers between devices, per_device(): lax.all_to_all(sent, 'z', split_axis=0, concat_axis=0, tiled=True)  6.71 us
    ppermute x1, starting transfers between devices, per_device(): across = lax.ppermute(side, TGT, links + [(b, a) for a, b in links])  5.65 us
    ppermute x1, starting transfers between devices, per_device(): gathered2 = lax.ppermute(gathered, 'yh', swap)  2.91 us
    ppermute x1, starting transfers between devices, per_device(): arrived = lax.ppermute(share, 'core', swap)  2.08 us
    pallas_call x1, Pallas kernels, source_payload(): pl.pallas_call(payload_kernel, in_specs=[pl.BlockSpec(memory_space=pltpu....  1.84 us
  transfers between devices with their start and end apart: 5, of which 2 were waited for; matrix products, arithmetic and copies ran while one was open for 1% of the time, Pallas kernels for 25%

profile of v3, /device:TPU:1, one launch (start us, length us, event | category | flops | bytes accessed | tf_op | source)
XLA Modules:
  0.0 81.2 jit_solution(11119773830995145744)
XLA Ops:
  0.0 1.8 %payload.1 = (bf16[8,192,128]{2,1,0:T(8,128)(2,1)}, bf16[8,512]{1,0:T(8,128)(2,1)}) custom-call(f32[4,2,4]{2,1,0:T(2,128)} %factor_ref.1, bf16[3,4,128]{2,1,0:T(4,128)(2,1)} %bitcast.15, f32[4,128]{1,0:T(4,128)} %weight_ref.1, f32[3,4,128]{2,1,0:T(4,128)} %bitcast.14, s32[4,128]{1,0:T(4,128)} %span_ref.1, s32[4,128]{1,0:T(4,128)} %patch_ref.1, ...), custom_call_target="tpu_custom_call" | custom-call | tf_op jit(solution)/shard_map/payload/pallas_call | solution.py:101
  1.8 9.0 %all-to-all-start = ((bf16[8,192,128]{2,1,0:T(8,128)(2,1)}), bf16[8,192,128]{2,1,0:T(8,128)(2,1)S(1)}, u32[]{:S(2)}, u32[]{:S(2)}) async-start(bf16[8,192,128]{2,1,0:T(8,128)(2,1)} %get-tuple-element.12), calls=%async_computation | async-start | bytes 786432 | tf_op jit(solution)/shard_map/all_to_all | solution.py:364
  10.9 5.7 %collective-permute-start = (bf16[8,512]{1,0:T(8,128)(2,1)}, bf16[8,512]{1,0:T(8,128)(2,1)S(1)}, u32[]{:S(2)}, u32[]{:S(2)}) collective-permute-start(bf16[8,512]{1,0:T(8,128)(2,1)} %get-tuple-element.11), channel_id=1, source_target_pairs={{8,16},{24,32},{40,48},{56,64},{72,80},{88,96},{104,112},{120,128}... | collective-permute-start | bytes 24584 | tf_op jit(solution)/shard_map/ppermute | solution.py:363
  16.5 0.7 constant_dynamic-update-slice_fusion.1
  17.2 1.1 %collective-permute-done = bf16[8,512]{1,0:T(8,128)(2,1)S(1)} collective-permute-done((bf16[8,512]{1,0:T(8,128)(2,1)}, bf16[8,512]{1,0:T(8,128)(2,1)S(1)}, u32[]{:S(2)}, u32[]{:S(2)}) %collective-permute-start) | collective-permute-done | bytes 8224 | tf_op jit(solution)/shard_map/ppermute | solution.py:363
  18.3 0.0 collective-permute-start.1
  18.3 6.7 %all-to-all-done.refs_3_ = bf16[8,192,128]{2,1,0:T(8,128)(2,1)S(1)} async-done(((bf16[8,192,128]{2,1,0:T(8,128)(2,1)}), bf16[8,192,128]{2,1,0:T(8,128)(2,1)S(1)}, u32[]{:S(2)}, u32[]{:S(2)}) %all-to-all-start) | async-done | bytes 393248 | tf_op jit(solution)/shard_map/all_to_all | solution.py:364
  25.1 2.9 %collective-permute-start.2 = (bf16[8,192,128]{2,1,0:T(8,128)(2,1)S(1)}, bf16[8,192,128]{2,1,0:T(8,128)(2,1)S(1)}, u32[]{:S(2)}, u32[]{:S(2)}) collective-permute-start(bf16[8,192,128]{2,1,0:T(8,128)(2,1)S(1)} %all-to-all-done.refs_3_), channel_id=1, source_target_pairs={{0,16},{16,0},{1,17},{17,1},{2,18},{18,2},{3,19},{19,3},{4,20},{20... | collective-permute-start | bytes 1179656 | tf_op jit(solution)/shard_map/ppermute | solution.py:371
  28.0 0.0 collective-permute-done.1.refs_2_
  28.0 13.9 %terms.3 = (f32[2,528,128]{2,1,0:T(8,128)S(1)}, f32[2,8,640]{2,1,0:T(8,128)S(1)}) custom-call(s32[1]{0:T(128)} %bitcast.refs_0_, bf16[16,512]{1,0:T(8,128)(2,1)S(1)} %constant_dynamic-update-slice_fusion.refs_1_, bf16[16,512]{1,0:T(8,128)(2,1)S(1)} %collective-permute-done.1.refs_2_, bf16[8,192,128]{2,1,0:T(8,128)(2,1)S(1)} %all-to-all-done.refs_3_), custom_call_target="tpu_custom_call" | custom-call | flops 4429185024 | bytes 1048576 | tf_op jit(solution)/shard_map/terms/pallas_call | solution.py:301
  41.9 0.0 collective-permute-done.2.refs_1_
  41.9 8.3 %terms.4 = (f32[1,528,128]{2,1,0:T(8,128)S(1)}, bf16[4608,128]{1,0:T(8,128)(2,1)S(1)}) custom-call(f32[2,8,640]{2,1,0:T(8,128)S(1)} %get-tuple-element.13.refs_0_, bf16[8,192,128]{2,1,0:T(8,128)(2,1)S(1)} %collective-permute-done.2.refs_1_, f32[2,528,128]{2,1,0:T(8,128)S(1)} %get-tuple-element.14.refs_2_), custom_call_target="tpu_custom_call" | custom-call | flops 2214592512 | bytes 1048576 | tf_op jit(solution)/shard_map/terms/pallas_call | solution.py:301
  50.3 2.1 %collective-permute-start.3 = (f32[1,528,128]{2,1,0:T(8,128)S(1)}, f32[1,528,128]{2,1,0:T(8,128)S(1)}, u32[]{:S(2)}, u32[]{:S(2)}) collective-permute-start(f32[1,528,128]{2,1,0:T(8,128)S(1)} %get-tuple-element.16), channel_id=1, source_target_pairs={{0,8},{8,0},{1,9},{9,1},{2,10},{10,2},{3,11},{11,3},{4,12},{12,4},... | collective-permute-start | bytes 811016 | tf_op jit(solution)/shard_map/ppermute | solution.py:375
  52.3 0.0 copy-start
  52.3 0.0 copy-start.1
  52.3 6.6 %terms.5 = f32[1,528,128]{2,1,0:T(8,128)S(1)} custom-call(f32[2,8,640]{2,1,0:T(8,128)S(1)} %get-tuple-element.13.refs_0_, bf16[4608,128]{1,0:T(8,128)(2,1)S(1)} %get-tuple-element.15.refs_1_, f32[2,528,128]{2,1,0:T(8,128)S(1)} %get-tuple-element.14.refs_2_), custom_call_target="tpu_custom_call" | custom-call | flops 2214592512 | bytes 1048576 | tf_op jit(solution)/shard_map/terms/pallas_call | solution.py:301
  59.0 0.0 collective-permute-done.3
  59.0 0.0 copy-done
  59.0 0.0 copy-done.1
  59.0 1.5 %band.1 = bf16[8,512,128]{2,1,0:T(8,128)(2,1)S(1)} custom-call(s32[8]{0:T(128)S(1)} %copy-done.1, f32[528,128]{1,0:T(8,128)S(1)} %bitcast.12, f32[528,128]{1,0:T(8,128)S(1)} %bitcast.11, f32[8,640]{1,0:T(8,128)S(1)} %slice_bitcast_fusion.side_ref, f32[8,512]{1,0:T(8,128)S(1)} %copy-done), custom_call_target="tpu_custom_call" | custom-call | tf_op jit(solution)/shard_map/band/pallas_call | solution.py:338
  60.5 19.8 %all_to_all.10 = bf16[8,512,128]{2,1,0:T(8,128)(2,1)S(1)} all-to-all(bf16[8,512,128]{2,1,0:T(8,128)(2,1)S(1)} %band.1), channel_id=1, replica_groups=mesh['z'=8,'yh'=2,'core'=2,'yl'=2,'x'=4] {'yl','x'}, dimensions={0} | all-to-all | bytes 2097152 | tf_op jit(solution)/shard_map/all_to_all | solution.py:381
  80.3 0.8 %convert_reduce_fusion = f32[512,128]{1,0:T(8,128)} fusion(bf16[8,512,128]{2,1,0:T(8,128)(2,1)S(1)} %all_to_all.10), kind=kLoop, calls=%fused_computation | loop fusion | flops 983040 | bytes 1310720 | tf_op jit(solution)/shard_map/reduce_sum | solution.py:382
  (2 shorter events, 0.0 us)
Async XLA Ops:
  1.8 23.2 %all-to-all-start = ((bf16[8,192,128]{2,1,0:T(8,128)(2,1)}), bf16[8,192,128]{2,1,0:T(8,128)(2,1)S(1)}, u32[]{:S(2)}, u32[]{:S(2)}) async-start(bf16[8,192,128]{2,1,0:T(8,128)(2,1)} %get-tuple-element.12), calls=%async_computation | async-start | bytes 786432 | tf_op jit(solution)/shard_map/all_to_all | solution.py:364
  10.9 7.5 %collective-permute-start = (bf16[8,512]{1,0:T(8,128)(2,1)}, bf16[8,512]{1,0:T(8,128)(2,1)S(1)}, u32[]{:S(2)}, u32[]{:S(2)}) collective-permute-start(bf16[8,512]{1,0:T(8,128)(2,1)} %get-tuple-element.11), channel_id=1, source_target_pairs={{8,16},{24,32},{40,48},{56,64},{72,80},{88,96},{104,112},{120,128}... | collective-permute-start | bytes 24584 | tf_op jit(solution)/shard_map/ppermute | solution.py:363
  18.3 9.6 %collective-permute-start.1 = (bf16[16,512]{1,0:T(8,128)(2,1)S(1)}, bf16[16,512]{1,0:T(8,128)(2,1)S(1)}, u32[]{:S(2)}, u32[]{:S(2)}) collective-permute-start(bf16[16,512]{1,0:T(8,128)(2,1)S(1)} %constant_dynamic-update-slice_fusion.refs_1_), channel_id=1, source_target_pairs={{0,8},{8,0},{1,9},{9,1},{2,10},{10,2},{3,11},{11,3},{4,12},{12,4},... | collective-permute-start | bytes 49160 | tf_op jit(solution)/shard_map/ppermute | solution.py:366
  25.1 16.8 %collective-permute-start.2 = (bf16[8,192,128]{2,1,0:T(8,128)(2,1)S(1)}, bf16[8,192,128]{2,1,0:T(8,128)(2,1)S(1)}, u32[]{:S(2)}, u32[]{:S(2)}) collective-permute-start(bf16[8,192,128]{2,1,0:T(8,128)(2,1)S(1)} %all-to-all-done.refs_3_), channel_id=1, source_target_pairs={{0,16},{16,0},{1,17},{17,1},{2,18},{18,2},{3,19},{19,3},{4,20},{20... | collective-permute-start | bytes 1179656 | tf_op jit(solution)/shard_map/ppermute | solution.py:371
  50.3 8.7 %collective-permute-start.3 = (f32[1,528,128]{2,1,0:T(8,128)S(1)}, f32[1,528,128]{2,1,0:T(8,128)S(1)}, u32[]{:S(2)}, u32[]{:S(2)}) collective-permute-start(f32[1,528,128]{2,1,0:T(8,128)S(1)} %get-tuple-element.16), channel_id=1, source_target_pairs={{0,8},{8,0},{1,9},{9,1},{2,10},{10,2},{3,11},{11,3},{4,12},{12,4},... | collective-permute-start | bytes 811016 | tf_op jit(solution)/shard_map/ppermute | solution.py:375
  52.3 6.6 %copy-start = (f32[8,512]{1,0:T(8,128)S(1)}, f32[8,512]{1,0:T(8,128)}, u32[]{:S(2)}) copy-start(f32[8,512]{1,0:T(8,128)} %band_ref.1) | copy-start | bytes 49156
  52.3 6.7 %copy-start.1 = (s32[8]{0:T(128)S(1)}, s32[8]{0:T(128)}, u32[]{:S(2)}) copy-start(s32[8]{0:T(128)} %offsets_ref.1) | copy-start | bytes 100

commit v4 on v3

--- a/solution.py
+++ b/solution.py
@@ -271,7 +271,7 @@
     tiles = 2 if first else 1
     count = sources.shape[-1]
     chunk = rounds * count + 16 * rounds
-    per_step = 2 if first else 4
+    per_step = 8 if make and not first else 4
     if make:
         chunks = sources.shape[0]
         source_spec = pl.BlockSpec((per_step,) + sources.shape[1:], lambda i: (i, 0, 0))

time: 81.5 us -> 80.6 us (0.989)
  no operation moved by 1% of the time
where the time goes in v4:
time: 80.6 us; the launch traced here: 80.2 us
  Pallas kernels  31.5 us (39%)
  blocking collectives  19.8 us (25%)
  starting transfers between devices  19.5 us (24%)
  waiting for transfers between devices  7.83 us (10%)
  other arithmetic  0.85 us (1%)
    pallas_call x3, Pallas kernels, kernel_sums(): pl.pallas_call(functools.partial(terms_kernel, first, make, rounds, contr...  28.1 us
    all_to_all x1, blocking collectives, per_device(): lax.all_to_all(shares, SRC, split_axis=0, concat_axis=0, tiled=True)  19.8 us
    all_to_all x1, starting transfers between devices, per_device(): lax.all_to_all(sent, 'z', split_axis=0, concat_axis=0, tiled=True)  9.02 us
    all_to_all x1, waiting for transfers between devices, per_device(): lax.all_to_all(sent, 'z', split_axis=0, concat_axis=0, tiled=True)  6.71 us
    ppermute x1, starting transfers between devices, per_device(): across = lax.ppermute(side, TGT, links + [(b, a) for a, b in links])  5.65 us
    ppermute x1, starting transfers between devices, per_device(): gathered2 = lax.ppermute(gathered, 'yh', swap)  2.91 us
    ppermute x1, starting transfers between devices, per_device(): arrived = lax.ppermute(share, 'core', swap)  1.9 us
    pallas_call x1, Pallas kernels, source_payload(): pl.pallas_call(payload_kernel, in_specs=[pl.BlockSpec(memory_space=pltpu....  1.84 us
  transfers between devices with their start and end apart: 5, of which 2 were waited for; matrix products, arithmetic and copies ran while one was open for 1% of the time, Pallas kernels for 25%

profile of v4, /device:TPU:1, one launch (start us, length us, event | category | flops | bytes accessed | tf_op | source)
XLA Modules:
  0.0 80.2 jit_solution(4278854700032164850)
XLA Ops:
  0.0 1.8 %payload.1 = (bf16[8,192,128]{2,1,0:T(8,128)(2,1)}, bf16[8,512]{1,0:T(8,128)(2,1)}) custom-call(f32[4,2,4]{2,1,0:T(2,128)} %factor_ref.1, bf16[3,4,128]{2,1,0:T(4,128)(2,1)} %bitcast.15, f32[4,128]{1,0:T(4,128)} %weight_ref.1, f32[3,4,128]{2,1,0:T(4,128)} %bitcast.14, s32[4,128]{1,0:T(4,128)} %span_ref.1, s32[4,128]{1,0:T(4,128)} %patch_ref.1, ...), custom_call_target="tpu_custom_call" | custom-call | tf_op jit(solution)/shard_map/payload/pallas_call | solution.py:101
  1.8 9.0 %all-to-all-start = ((bf16[8,192,128]{2,1,0:T(8,128)(2,1)}), bf16[8,192,128]{2,1,0:T(8,128)(2,1)S(1)}, u32[]{:S(2)}, u32[]{:S(2)}) async-start(bf16[8,192,128]{2,1,0:T(8,128)(2,1)} %get-tuple-element.12), calls=%async_computation | async-start | bytes 786432 | tf_op jit(solution)/shard_map/all_to_all | solution.py:364
  10.9 5.7 %collective-permute-start = (bf16[8,512]{1,0:T(8,128)(2,1)}, bf16[8,512]{1,0:T(8,128)(2,1)S(1)}, u32[]{:S(2)}, u32[]{:S(2)}) collective-permute-start(bf16[8,512]{1,0:T(8,128)(2,1)} %get-tuple-element.11), channel_id=1, source_target_pairs={{8,16},{24,32},{40,48},{56,64},{72,80},{88,96},{104,112},{120,128}... | collective-permute-start | bytes 24584 | tf_op jit(solution)/shard_map/ppermute | solution.py:363
  16.5 0.7 constant_dynamic-update-slice_fusion.1
  17.2 1.1 %collective-permute-done = bf16[8,512]{1,0:T(8,128)(2,1)S(1)} collective-permute-done((bf16[8,512]{1,0:T(8,128)(2,1)}, bf16[8,512]{1,0:T(8,128)(2,1)S(1)}, u32[]{:S(2)}, u32[]{:S(2)}) %collective-permute-start) | collective-permute-done | bytes 8224 | tf_op jit(solution)/shard_map/ppermute | solution.py:363
  18.3 0.0 collective-permute-start.1
  18.3 6.7 %all-to-all-done.refs_3_ = bf16[8,192,128]{2,1,0:T(8,128)(2,1)S(1)} async-done(((bf16[8,192,128]{2,1,0:T(8,128)(2,1)}), bf16[8,192,128]{2,1,0:T(8,128)(2,1)S(1)}, u32[]{:S(2)}, u32[]{:S(2)}) %all-to-all-start) | async-done | bytes 393248 | tf_op jit(solution)/shard_map/all_to_all | solution.py:364
  25.1 2.9 %collective-permute-start.2 = (bf16[8,192,128]{2,1,0:T(8,128)(2,1)S(1)}, bf16[8,192,128]{2,1,0:T(8,128)(2,1)S(1)}, u32[]{:S(2)}, u32[]{:S(2)}) collective-permute-start(bf16[8,192,128]{2,1,0:T(8,128)(2,1)S(1)} %all-to-all-done.refs_3_), channel_id=1, source_target_pairs={{0,16},{16,0},{1,17},{17,1},{2,18},{18,2},{3,19},{19,3},{4,20},{20... | collective-permute-start | bytes 1179656 | tf_op jit(solution)/shard_map/ppermute | solution.py:371
  28.0 0.0 collective-permute-done.1.refs_2_
  28.0 13.6 %terms.3 = (f32[2,528,128]{2,1,0:T(8,128)S(1)}, f32[2,8,640]{2,1,0:T(8,128)S(1)}) custom-call(s32[1]{0:T(128)} %bitcast.refs_0_, bf16[16,512]{1,0:T(8,128)(2,1)S(1)} %constant_dynamic-update-slice_fusion.refs_1_, bf16[16,512]{1,0:T(8,128)(2,1)S(1)} %collective-permute-done.1.refs_2_, bf16[8,192,128]{2,1,0:T(8,128)(2,1)S(1)} %all-to-all-done.refs_3_), custom_call_target="tpu_custom_call" | custom-call | flops 4429185024 | bytes 1048576 | tf_op jit(solution)/shard_map/terms/pallas_call | solution.py:301
  41.6 0.0 collective-permute-done.2.refs_1_
  41.6 7.9 %terms.4 = (f32[1,528,128]{2,1,0:T(8,128)S(1)}, bf16[4608,128]{1,0:T(8,128)(2,1)S(1)}) custom-call(f32[2,8,640]{2,1,0:T(8,128)S(1)} %get-tuple-element.13.refs_0_, bf16[8,192,128]{2,1,0:T(8,128)(2,1)S(1)} %collective-permute-done.2.refs_1_, f32[2,528,128]{2,1,0:T(8,128)S(1)} %get-tuple-element.14.refs_2_), custom_call_target="tpu_custom_call" | custom-call | flops 2214592512 | bytes 1048576 | tf_op jit(solution)/shard_map/terms/pallas_call | solution.py:301
  49.5 1.9 %collective-permute-start.3 = (f32[1,528,128]{2,1,0:T(8,128)S(1)}, f32[1,528,128]{2,1,0:T(8,128)S(1)}, u32[]{:S(2)}, u32[]{:S(2)}) collective-permute-start(f32[1,528,128]{2,1,0:T(8,128)S(1)} %get-tuple-element.16), channel_id=1, source_target_pairs={{0,8},{8,0},{1,9},{9,1},{2,10},{10,2},{3,11},{11,3},{4,12},{12,4},... | collective-permute-start | bytes 811016 | tf_op jit(solution)/shard_map/ppermute | solution.py:375
  51.4 0.0 copy-start
  51.4 0.0 copy-start.1
  51.4 6.6 %terms.5 = f32[1,528,128]{2,1,0:T(8,128)S(1)} custom-call(f32[2,8,640]{2,1,0:T(8,128)S(1)} %get-tuple-element.13.refs_0_, bf16[4608,128]{1,0:T(8,128)(2,1)S(1)} %get-tuple-element.15.refs_1_, f32[2,528,128]{2,1,0:T(8,128)S(1)} %get-tuple-element.14.refs_2_), custom_call_target="tpu_custom_call" | custom-call | flops 2214592512 | bytes 1048576 | tf_op jit(solution)/shard_map/terms/pallas_call | solution.py:301
  58.0 0.0 collective-permute-done.3
  58.0 0.0 copy-done
  58.1 0.0 copy-done.1
  58.1 1.5 %band.1 = bf16[8,512,128]{2,1,0:T(8,128)(2,1)S(1)} custom-call(s32[8]{0:T(128)S(1)} %copy-done.1, f32[528,128]{1,0:T(8,128)S(1)} %bitcast.12, f32[528,128]{1,0:T(8,128)S(1)} %bitcast.11, f32[8,640]{1,0:T(8,128)S(1)} %slice_bitcast_fusion.side_ref, f32[8,512]{1,0:T(8,128)S(1)} %copy-done), custom_call_target="tpu_custom_call" | custom-call | tf_op jit(solution)/shard_map/band/pallas_call | solution.py:338
  59.6 19.8 %all_to_all.10 = bf16[8,512,128]{2,1,0:T(8,128)(2,1)S(1)} all-to-all(bf16[8,512,128]{2,1,0:T(8,128)(2,1)S(1)} %band.1), channel_id=1, replica_groups=mesh['z'=8,'yh'=2,'core'=2,'yl'=2,'x'=4] {'yl','x'}, dimensions={0} | all-to-all | bytes 2097152 | tf_op jit(solution)/shard_map/all_to_all | solution.py:381
  79.4 0.8 %convert_reduce_fusion = f32[512,128]{1,0:T(8,128)} fusion(bf16[8,512,128]{2,1,0:T(8,128)(2,1)S(1)} %all_to_all.10), kind=kLoop, calls=%fused_computation | loop fusion | flops 983040 | bytes 1310720 | tf_op jit(solution)/shard_map/reduce_sum | solution.py:382
  (2 shorter events, 0.0 us)
Async XLA Ops:
  1.8 23.2 %all-to-all-start = ((bf16[8,192,128]{2,1,0:T(8,128)(2,1)}), bf16[8,192,128]{2,1,0:T(8,128)(2,1)S(1)}, u32[]{:S(2)}, u32[]{:S(2)}) async-start(bf16[8,192,128]{2,1,0:T(8,128)(2,1)} %get-tuple-element.12), calls=%async_computation | async-start | bytes 786432 | tf_op jit(solution)/shard_map/all_to_all | solution.py:364
  10.9 7.5 %collective-permute-start = (bf16[8,512]{1,0:T(8,128)(2,1)}, bf16[8,512]{1,0:T(8,128)(2,1)S(1)}, u32[]{:S(2)}, u32[]{:S(2)}) collective-permute-start(bf16[8,512]{1,0:T(8,128)(2,1)} %get-tuple-element.11), channel_id=1, source_target_pairs={{8,16},{24,32},{40,48},{56,64},{72,80},{88,96},{104,112},{120,128}... | collective-permute-start | bytes 24584 | tf_op jit(solution)/shard_map/ppermute | solution.py:363
  18.3 9.6 %collective-permute-start.1 = (bf16[16,512]{1,0:T(8,128)(2,1)S(1)}, bf16[16,512]{1,0:T(8,128)(2,1)S(1)}, u32[]{:S(2)}, u32[]{:S(2)}) collective-permute-start(bf16[16,512]{1,0:T(8,128)(2,1)S(1)} %constant_dynamic-update-slice_fusion.refs_1_), channel_id=1, source_target_pairs={{0,8},{8,0},{1,9},{9,1},{2,10},{10,2},{3,11},{11,3},{4,12},{12,4},... | collective-permute-start | bytes 49160 | tf_op jit(solution)/shard_map/ppermute | solution.py:366
  25.1 16.5 %collective-permute-start.2 = (bf16[8,192,128]{2,1,0:T(8,128)(2,1)S(1)}, bf16[8,192,128]{2,1,0:T(8,128)(2,1)S(1)}, u32[]{:S(2)}, u32[]{:S(2)}) collective-permute-start(bf16[8,192,128]{2,1,0:T(8,128)(2,1)S(1)} %all-to-all-done.refs_3_), channel_id=1, source_target_pairs={{0,16},{16,0},{1,17},{17,1},{2,18},{18,2},{3,19},{19,3},{4,20},{20... | collective-permute-start | bytes 1179656 | tf_op jit(solution)/shard_map/ppermute | solution.py:371
  49.5 8.5 %collective-permute-start.3 = (f32[1,528,128]{2,1,0:T(8,128)S(1)}, f32[1,528,128]{2,1,0:T(8,128)S(1)}, u32[]{:S(2)}, u32[]{:S(2)}) collective-permute-start(f32[1,528,128]{2,1,0:T(8,128)S(1)} %get-tuple-element.16), channel_id=1, source_target_pairs={{0,8},{8,0},{1,9},{9,1},{2,10},{10,2},{3,11},{11,3},{4,12},{12,4},... | collective-permute-start | bytes 811016 | tf_op jit(solution)/shard_map/ppermute | solution.py:375
  51.4 6.7 %copy-start = (f32[8,512]{1,0:T(8,128)S(1)}, f32[8,512]{1,0:T(8,128)}, u32[]{:S(2)}) copy-start(f32[8,512]{1,0:T(8,128)} %band_ref.1) | copy-start | bytes 49156
  51.4 6.7 %copy-start.1 = (s32[8]{0:T(128)S(1)}, s32[8]{0:T(128)}, u32[]{:S(2)}) copy-start(s32[8]{0:T(128)} %offsets_ref.1) | copy-start | bytes 100

commit v5 on v4

--- a/solution.py
+++ b/solution.py
@@ -378,7 +378,7 @@
     source_count = rounds * src_weight.shape[1] * blocks * groups
     scale = TURN / math.sqrt(source_count)
     shares = band_shares(groups, scale, offsets, own[0], arrived[0], wide[0], band)
-    shares = lax.all_to_all(shares, SRC, split_axis=0, concat_axis=0, tiled=True)
+    shares = lax.all_to_all(shares, SRC[::-1], split_axis=0, concat_axis=0, tiled=True)
     return jnp.sum(shares.astype(jnp.float32), axis=0)
 
 

time: 80.6 us -> 79.1 us (0.981)
  blocking collectives: 19.8 us -> 18.3 us
    all_to_all x1, blocking collectives: 19.8 us -> 18.3 us  [per_device(): lax.all_to_all(shares, SRC[::-1], split_axis=0, concat_axis=0, tiled=True)]
  transfers between devices with their start and end apart: 5 -> 5, of which waited for: 2 -> 2; matrix products, arithmetic and copies ran while one was open for 1% -> 1% of each run, Pallas kernels for 25% -> 26%
where the time goes in v5:
time: 79.1 us; the launch traced here: 78.7 us
  Pallas kernels  31.5 us (40%)
  starting transfers between devices  19.5 us (25%)
  blocking collectives  18.3 us (23%)
  waiting for transfers between devices  7.83 us (10%)
  other arithmetic  0.85 us (1%)
    pallas_call x3, Pallas kernels, kernel_sums(): pl.pallas_call(functools.partial(terms_kernel, first, make, rounds, contr...  28.1 us
    all_to_all x1, blocking collectives, per_device(): lax.all_to_all(shares, SRC[::-1], split_axis=0, concat_axis=0, tiled=True)  18.3 us
    all_to_all x1, starting transfers between devices, per_device(): lax.all_to_all(sent, 'z', split_axis=0, concat_axis=0, tiled=True)  9.02 us
    all_to_all x1, waiting for transfers between devices, per_device(): lax.all_to_all(sent, 'z', split_axis=0, concat_axis=0, tiled=True)  6.71 us
    ppermute x1, starting transfers between devices, per_device(): across = lax.ppermute(side, TGT, links + [(b, a) for a, b in links])  5.65 us
    ppermute x1, starting transfers between devices, per_device(): gathered2 = lax.ppermute(gathered, 'yh', swap)  2.91 us
    ppermute x1, starting transfers between devices, per_device(): arrived = lax.ppermute(share, 'core', swap)  1.9 us
    pallas_call x1, Pallas kernels, source_payload(): pl.pallas_call(payload_kernel, in_specs=[pl.BlockSpec(memory_space=pltpu....  1.84 us
  transfers between devices with their start and end apart: 5, of which 2 were waited for; matrix products, arithmetic and copies ran while one was open for 1% of the time, Pallas kernels for 26%

profile of v5, /device:TPU:1, one launch (start us, length us, event | category | flops | bytes accessed | tf_op | source)
XLA Modules:
  0.0 78.7 jit_solution(4829319246210288770)
XLA Ops:
  0.0 1.8 %payload.1 = (bf16[8,192,128]{2,1,0:T(8,128)(2,1)}, bf16[8,512]{1,0:T(8,128)(2,1)}) custom-call(f32[4,2,4]{2,1,0:T(2,128)} %factor_ref.1, bf16[3,4,128]{2,1,0:T(4,128)(2,1)} %bitcast.15, f32[4,128]{1,0:T(4,128)} %weight_ref.1, f32[3,4,128]{2,1,0:T(4,128)} %bitcast.14, s32[4,128]{1,0:T(4,128)} %span_ref.1, s32[4,128]{1,0:T(4,128)} %patch_ref.1, ...), custom_call_target="tpu_custom_call" | custom-call | tf_op jit(solution)/shard_map/payload/pallas_call | solution.py:101
  1.8 9.0 %all-to-all-start = ((bf16[8,192,128]{2,1,0:T(8,128)(2,1)}), bf16[8,192,128]{2,1,0:T(8,128)(2,1)S(1)}, u32[]{:S(2)}, u32[]{:S(2)}) async-start(bf16[8,192,128]{2,1,0:T(8,128)(2,1)} %get-tuple-element.12), calls=%async_computation | async-start | bytes 786432 | tf_op jit(solution)/shard_map/all_to_all | solution.py:364
  10.9 5.7 %collective-permute-start = (bf16[8,512]{1,0:T(8,128)(2,1)}, bf16[8,512]{1,0:T(8,128)(2,1)S(1)}, u32[]{:S(2)}, u32[]{:S(2)}) collective-permute-start(bf16[8,512]{1,0:T(8,128)(2,1)} %get-tuple-element.11), channel_id=1, source_target_pairs={{8,16},{24,32},{40,48},{56,64},{72,80},{88,96},{104,112},{120,128}... | collective-permute-start | bytes 24584 | tf_op jit(solution)/shard_map/ppermute | solution.py:363
  16.5 0.7 constant_dynamic-update-slice_fusion.1
  17.2 1.1 %collective-permute-done = bf16[8,512]{1,0:T(8,128)(2,1)S(1)} collective-permute-done((bf16[8,512]{1,0:T(8,128)(2,1)}, bf16[8,512]{1,0:T(8,128)(2,1)S(1)}, u32[]{:S(2)}, u32[]{:S(2)}) %collective-permute-start) | collective-permute-done | bytes 8224 | tf_op jit(solution)/shard_map/ppermute | solution.py:363
  18.3 0.0 collective-permute-start.1
  18.3 6.7 %all-to-all-done.refs_3_ = bf16[8,192,128]{2,1,0:T(8,128)(2,1)S(1)} async-done(((bf16[8,192,128]{2,1,0:T(8,128)(2,1)}), bf16[8,192,128]{2,1,0:T(8,128)(2,1)S(1)}, u32[]{:S(2)}, u32[]{:S(2)}) %all-to-all-start) | async-done | bytes 393248 | tf_op jit(solution)/shard_map/all_to_all | solution.py:364
  25.1 2.9 %collective-permute-start.2 = (bf16[8,192,128]{2,1,0:T(8,128)(2,1)S(1)}, bf16[8,192,128]{2,1,0:T(8,128)(2,1)S(1)}, u32[]{:S(2)}, u32[]{:S(2)}) collective-permute-start(bf16[8,192,128]{2,1,0:T(8,128)(2,1)S(1)} %all-to-all-done.refs_3_), channel_id=1, source_target_pairs={{0,16},{16,0},{1,17},{17,1},{2,18},{18,2},{3,19},{19,3},{4,20},{20... | collective-permute-start | bytes 1179656 | tf_op jit(solution)/shard_map/ppermute | solution.py:371
  28.0 0.0 collective-permute-done.1.refs_2_
  28.0 13.6 %terms.3 = (f32[2,528,128]{2,1,0:T(8,128)S(1)}, f32[2,8,640]{2,1,0:T(8,128)S(1)}) custom-call(s32[1]{0:T(128)} %bitcast.refs_0_, bf16[16,512]{1,0:T(8,128)(2,1)S(1)} %constant_dynamic-update-slice_fusion.refs_1_, bf16[16,512]{1,0:T(8,128)(2,1)S(1)} %collective-permute-done.1.refs_2_, bf16[8,192,128]{2,1,0:T(8,128)(2,1)S(1)} %all-to-all-done.refs_3_), custom_call_target="tpu_custom_call" | custom-call | flops 4429185024 | bytes 1048576 | tf_op jit(solution)/shard_map/terms/pallas_call | solution.py:301
  41.6 0.0 collective-permute-done.2.refs_1_
  41.6 7.9 %terms.4 = (f32[1,528,128]{2,1,0:T(8,128)S(1)}, bf16[4608,128]{1,0:T(8,128)(2,1)S(1)}) custom-call(f32[2,8,640]{2,1,0:T(8,128)S(1)} %get-tuple-element.13.refs_0_, bf16[8,192,128]{2,1,0:T(8,128)(2,1)S(1)} %collective-permute-done.2.refs_1_, f32[2,528,128]{2,1,0:T(8,128)S(1)} %get-tuple-element.14.refs_2_), custom_call_target="tpu_custom_call" | custom-call | flops 2214592512 | bytes 1048576 | tf_op jit(solution)/shard_map/terms/pallas_call | solution.py:301
  49.5 1.9 %collective-permute-start.3 = (f32[1,528,128]{2,1,0:T(8,128)S(1)}, f32[1,528,128]{2,1,0:T(8,128)S(1)}, u32[]{:S(2)}, u32[]{:S(2)}) collective-permute-start(f32[1,528,128]{2,1,0:T(8,128)S(1)} %get-tuple-element.16), channel_id=1, source_target_pairs={{0,8},{8,0},{1,9},{9,1},{2,10},{10,2},{3,11},{11,3},{4,12},{12,4},... | collective-permute-start | bytes 811016 | tf_op jit(solution)/shard_map/ppermute | solution.py:375
  51.4 0.0 copy-start
  51.4 0.0 copy-start.1
  51.4 6.6 %terms.5 = f32[1,528,128]{2,1,0:T(8,128)S(1)} custom-call(f32[2,8,640]{2,1,0:T(8,128)S(1)} %get-tuple-element.13.refs_0_, bf16[4608,128]{1,0:T(8,128)(2,1)S(1)} %get-tuple-element.15.refs_1_, f32[2,528,128]{2,1,0:T(8,128)S(1)} %get-tuple-element.14.refs_2_), custom_call_target="tpu_custom_call" | custom-call | flops 2214592512 | bytes 1048576 | tf_op jit(solution)/shard_map/terms/pallas_call | solution.py:301
  58.0 0.0 collective-permute-done.3
  58.0 0.0 copy-done
  58.1 0.0 copy-done.1
  58.1 1.5 %band.1 = bf16[8,512,128]{2,1,0:T(8,128)(2,1)S(1)} custom-call(s32[8]{0:T(128)S(1)} %copy-done.1, f32[528,128]{1,0:T(8,128)S(1)} %bitcast.12, f32[528,128]{1,0:T(8,128)S(1)} %bitcast.11, f32[8,640]{1,0:T(8,128)S(1)} %slice_bitcast_fusion.side_ref, f32[8,512]{1,0:T(8,128)S(1)} %copy-done), custom_call_target="tpu_custom_call" | custom-call | tf_op jit(solution)/shard_map/band/pallas_call | solution.py:338
  59.6 18.3 %all_to_all.10 = bf16[8,512,128]{2,1,0:T(8,128)(2,1)S(1)} all-to-all(bf16[8,512,128]{2,1,0:T(8,128)(2,1)S(1)} %band.1), channel_id=1, replica_groups=mesh['z'=8,'yh'=2,'core'=2,'yl'=2,'x'=4] {'x','yl'}, dimensions={0} | all-to-all | bytes 2097152 | tf_op jit(solution)/shard_map/all_to_all | solution.py:381
  77.9 0.8 %convert_reduce_fusion = f32[512,128]{1,0:T(8,128)} fusion(bf16[8,512,128]{2,1,0:T(8,128)(2,1)S(1)} %all_to_all.10), kind=kLoop, calls=%fused_computation | loop fusion | flops 983040 | bytes 1310720 | tf_op jit(solution)/shard_map/reduce_sum | solution.py:382
  (2 shorter events, 0.0 us)
Async XLA Ops:
  1.8 23.2 %all-to-all-start = ((bf16[8,192,128]{2,1,0:T(8,128)(2,1)}), bf16[8,192,128]{2,1,0:T(8,128)(2,1)S(1)}, u32[]{:S(2)}, u32[]{:S(2)}) async-start(bf16[8,192,128]{2,1,0:T(8,128)(2,1)} %get-tuple-element.12), calls=%async_computation | async-start | bytes 786432 | tf_op jit(solution)/shard_map/all_to_all | solution.py:364
  10.9 7.5 %collective-permute-start = (bf16[8,512]{1,0:T(8,128)(2,1)}, bf16[8,512]{1,0:T(8,128)(2,1)S(1)}, u32[]{:S(2)}, u32[]{:S(2)}) collective-permute-start(bf16[8,512]{1,0:T(8,128)(2,1)} %get-tuple-element.11), channel_id=1, source_target_pairs={{8,16},{24,32},{40,48},{56,64},{72,80},{88,96},{104,112},{120,128}... | collective-permute-start | bytes 24584 | tf_op jit(solution)/shard_map/ppermute | solution.py:363
  18.3 9.6 %collective-permute-start.1 = (bf16[16,512]{1,0:T(8,128)(2,1)S(1)}, bf16[16,512]{1,0:T(8,128)(2,1)S(1)}, u32[]{:S(2)}, u32[]{:S(2)}) collective-permute-start(bf16[16,512]{1,0:T(8,128)(2,1)S(1)} %constant_dynamic-update-slice_fusion.refs_1_), channel_id=1, source_target_pairs={{0,8},{8,0},{1,9},{9,1},{2,10},{10,2},{3,11},{11,3},{4,12},{12,4},... | collective-permute-start | bytes 49160 | tf_op jit(solution)/shard_map/ppermute | solution.py:366
  25.1 16.5 %collective-permute-start.2 = (bf16[8,192,128]{2,1,0:T(8,128)(2,1)S(1)}, bf16[8,192,128]{2,1,0:T(8,128)(2,1)S(1)}, u32[]{:S(2)}, u32[]{:S(2)}) collective-permute-start(bf16[8,192,128]{2,1,0:T(8,128)(2,1)S(1)} %all-to-all-done.refs_3_), channel_id=1, source_target_pairs={{0,16},{16,0},{1,17},{17,1},{2,18},{18,2},{3,19},{19,3},{4,20},{20... | collective-permute-start | bytes 1179656 | tf_op jit(solution)/shard_map/ppermute | solution.py:371
  49.5 8.5 %collective-permute-start.3 = (f32[1,528,128]{2,1,0:T(8,128)S(1)}, f32[1,528,128]{2,1,0:T(8,128)S(1)}, u32[]{:S(2)}, u32[]{:S(2)}) collective-permute-start(f32[1,528,128]{2,1,0:T(8,128)S(1)} %get-tuple-element.16), channel_id=1, source_target_pairs={{0,8},{8,0},{1,9},{9,1},{2,10},{10,2},{3,11},{11,3},{4,12},{12,4},... | collective-permute-start | bytes 811016 | tf_op jit(solution)/shard_map/ppermute | solution.py:375
  51.4 6.7 %copy-start = (f32[8,512]{1,0:T(8,128)S(1)}, f32[8,512]{1,0:T(8,128)}, u32[]{:S(2)}) copy-start(f32[8,512]{1,0:T(8,128)} %band_ref.1) | copy-start | bytes 49156
  51.4 6.7 %copy-start.1 = (s32[8]{0:T(128)S(1)}, s32[8]{0:T(128)}, u32[]{:S(2)}) copy-start(s32[8]{0:T(128)} %offsets_ref.1) | copy-start | bytes 100

commit v6 on v5

--- a/solution.py
+++ b/solution.py
@@ -15,7 +15,8 @@
 TURN = WAVE / (2.0 * math.pi)
 TURN_SQ = TURN * TURN
 
-TGT = ("z", "yh", "core")
+LINE = ("zl", "zh")
+TGT = ("zh", "zl", "yh", "core")
 SRC = ("yl", "x")
 
 
@@ -351,7 +352,7 @@
 ):
     rows = tgt_points.shape[1]
     rounds, columns, controls = ctrl_coef.shape
-    zs = lax.axis_size("z")
+    zs = lax.axis_size(LINE)
     groups = lax.axis_size(SRC)
     blocks = lax.axis_size(TGT)
     swap = [(0, 1), (1, 0)]
@@ -361,7 +362,7 @@
     )
     links = [(k, k + 1) for k in range(1, blocks - 1, 2)]
     across = lax.ppermute(side, TGT, links + [(b, a) for a, b in links])
-    gathered = lax.all_to_all(sent, "z", split_axis=0, concat_axis=0, tiled=True)
+    gathered = lax.all_to_all(sent, LINE, split_axis=0, concat_axis=0, tiled=True)
     block = jnp.concatenate([side, across], axis=0)
     other = lax.ppermute(block, "core", swap)
     core = lax.axis_index("core").astype(jnp.int32).reshape(1)
@@ -383,7 +384,7 @@
 
 
 def solution(mesh):
-    mesh = Mesh(mesh.devices.reshape(8, 2, 2, 2, 4), ("z", "yh", "core", "yl", "x"))
+    mesh = Mesh(mesh.devices.reshape(2, 4, 2, 2, 2, 4), ("zh", "zl", "yh", "core", "yl", "x"))
     both = TGT + SRC
     in_specs = (
         P(None, TGT),

time: 79.1 us -> 77.7 us (0.982)
  the two profiles are of different devices: /device:TPU:1 before, /device:TPU:32 now
where the time goes in v6:
time: 77.7 us; the launch traced here: 77.4 us
  Pallas kernels  31.7 us (41%)
  blocking collectives  20 us (26%)
  starting transfers between devices  15.5 us (20%)
  waiting for transfers between devices  8.44 us (11%)
  other arithmetic  0.85 us (1%)
    pallas_call x3, Pallas kernels, kernel_sums(): pl.pallas_call(functools.partial(terms_kernel, first, make, rounds, contr...  28.4 us
    all_to_all x1, blocking collectives, per_device(): lax.all_to_all(shares, SRC[::-1], split_axis=0, concat_axis=0, tiled=True)  20 us
    all_to_all x1, starting transfers between devices, per_device(): lax.all_to_all(sent, LINE, split_axis=0, concat_axis=0, tiled=True)  8.57 us
    all_to_all x1, waiting for transfers between devices, per_device(): lax.all_to_all(sent, LINE, split_axis=0, concat_axis=0, tiled=True)  4.52 us
    ppermute x1, waiting for transfers between devices, per_device(): across = lax.ppermute(side, TGT, links + [(b, a) for a, b in links])  3.91 us
    ppermute x1, starting transfers between devices, per_device(): across = lax.ppermute(side, TGT, links + [(b, a) for a, b in links])  3.69 us
    ppermute x1, starting transfers between devices, per_device(): gathered2 = lax.ppermute(gathered, 'yh', swap)  3.19 us
    pallas_call x1, Pallas kernels, source_payload(): pl.pallas_call(payload_kernel, in_specs=[pl.BlockSpec(memory_space=pltpu....  1.84 us
  transfers between devices with their start and end apart: 5, of which 2 were waited for; matrix products, arithmetic and copies ran while one was open for 1% of the time, Pallas kernels for 26%

profile of v6, /device:TPU:32, one launch (start us, length us, event | category | flops | bytes accessed | tf_op | source)
XLA Modules:
  0.0 77.4 jit_solution(11738252249900174996)
XLA Ops:
  0.0 1.8 %payload.1 = (bf16[8,192,128]{2,1,0:T(8,128)(2,1)}, bf16[8,512]{1,0:T(8,128)(2,1)}) custom-call(f32[4,2,4]{2,1,0:T(2,128)} %factor_ref.1, bf16[3,4,128]{2,1,0:T(4,128)(2,1)} %bitcast.15, f32[4,128]{1,0:T(4,128)} %weight_ref.1, f32[3,4,128]{2,1,0:T(4,128)} %bitcast.14, s32[4,128]{1,0:T(4,128)} %span_ref.1, s32[4,128]{1,0:T(4,128)} %patch_ref.1, ...), custom_call_target="tpu_custom_call" | custom-call | tf_op jit(solution)/shard_map/payload/pallas_call | solution.py:102
  1.8 8.6 %all-to-all-start = ((bf16[8,192,128]{2,1,0:T(8,128)(2,1)}), bf16[8,192,128]{2,1,0:T(8,128)(2,1)S(1)}, u32[]{:S(2)}, u32[]{:S(2)}) async-start(bf16[8,192,128]{2,1,0:T(8,128)(2,1)} %get-tuple-element.12), calls=%async_computation | async-start | bytes 786432 | tf_op jit(solution)/shard_map/all_to_all | solution.py:365
  10.4 3.7 %collective-permute-start = (bf16[8,512]{1,0:T(8,128)(2,1)}, bf16[8,512]{1,0:T(8,128)(2,1)S(1)}, u32[]{:S(2)}, u32[]{:S(2)}) collective-permute-start(bf16[8,512]{1,0:T(8,128)(2,1)} %get-tuple-element.11), channel_id=1, source_target_pairs={{8,16},{24,32},{40,48},{56,64},{72,80},{88,96},{104,112},{120,128}... | collective-permute-start | bytes 24584 | tf_op jit(solution)/shard_map/ppermute | solution.py:364
  14.1 0.7 constant_dynamic-update-slice_fusion.1
  14.8 3.9 %collective-permute-done = bf16[8,512]{1,0:T(8,128)(2,1)S(1)} collective-permute-done((bf16[8,512]{1,0:T(8,128)(2,1)}, bf16[8,512]{1,0:T(8,128)(2,1)S(1)}, u32[]{:S(2)}, u32[]{:S(2)}) %collective-permute-start) | collective-permute-done | bytes 8224 | tf_op jit(solution)/shard_map/ppermute | solution.py:364
  18.7 0.0 collective-permute-start.1
  18.7 4.5 %all-to-all-done.refs_3_ = bf16[8,192,128]{2,1,0:T(8,128)(2,1)S(1)} async-done(((bf16[8,192,128]{2,1,0:T(8,128)(2,1)}), bf16[8,192,128]{2,1,0:T(8,128)(2,1)S(1)}, u32[]{:S(2)}, u32[]{:S(2)}) %all-to-all-start) | async-done | bytes 393248 | tf_op jit(solution)/shard_map/all_to_all | solution.py:365
  23.3 3.2 %collective-permute-start.2 = (bf16[8,192,128]{2,1,0:T(8,128)(2,1)S(1)}, bf16[8,192,128]{2,1,0:T(8,128)(2,1)S(1)}, u32[]{:S(2)}, u32[]{:S(2)}) collective-permute-start(bf16[8,192,128]{2,1,0:T(8,128)(2,1)S(1)} %all-to-all-done.refs_3_), channel_id=1, source_target_pairs={{0,16},{16,0},{1,17},{17,1},{2,18},{18,2},{3,19},{19,3},{4,20},{20... | collective-permute-start | bytes 1179656 | tf_op jit(solution)/shard_map/ppermute | solution.py:372
  26.5 0.0 collective-permute-done.1.refs_2_
  26.5 13.6 %terms.3 = (f32[2,528,128]{2,1,0:T(8,128)S(1)}, f32[2,8,640]{2,1,0:T(8,128)S(1)}) custom-call(s32[1]{0:T(128)} %bitcast.refs_0_, bf16[16,512]{1,0:T(8,128)(2,1)S(1)} %constant_dynamic-update-slice_fusion.refs_1_, bf16[16,512]{1,0:T(8,128)(2,1)S(1)} %collective-permute-done.1.refs_2_, bf16[8,192,128]{2,1,0:T(8,128)(2,1)S(1)} %all-to-all-done.refs_3_), custom_call_target="tpu_custom_call" | custom-call | flops 4429185024 | bytes 1048576 | tf_op jit(solution)/shard_map/terms/pallas_call | solution.py:302
  40.1 0.0 collective-permute-done.2.refs_1_
  40.1 7.9 %terms.4 = (f32[1,528,128]{2,1,0:T(8,128)S(1)}, bf16[4608,128]{1,0:T(8,128)(2,1)S(1)}) custom-call(f32[2,8,640]{2,1,0:T(8,128)S(1)} %get-tuple-element.13.refs_0_, bf16[8,192,128]{2,1,0:T(8,128)(2,1)S(1)} %collective-permute-done.2.refs_1_, f32[2,528,128]{2,1,0:T(8,128)S(1)} %get-tuple-element.14.refs_2_), custom_call_target="tpu_custom_call" | custom-call | flops 2214592512 | bytes 1048576 | tf_op jit(solution)/shard_map/terms/pallas_call | solution.py:302
  48.0 0.1 collective-permute-start.3
  48.1 0.0 copy-start
  48.1 0.0 copy-start.1
  48.1 6.9 %terms.5 = f32[1,528,128]{2,1,0:T(8,128)S(1)} custom-call(f32[2,8,640]{2,1,0:T(8,128)S(1)} %get-tuple-element.13.refs_0_, bf16[4608,128]{1,0:T(8,128)(2,1)S(1)} %get-tuple-element.15.refs_1_, f32[2,528,128]{2,1,0:T(8,128)S(1)} %get-tuple-element.14.refs_2_), custom_call_target="tpu_custom_call" | custom-call | flops 2214592512 | bytes 1048576 | tf_op jit(solution)/shard_map/terms/pallas_call | solution.py:302
  55.0 0.0 collective-permute-done.3
  55.0 0.0 copy-done
  55.0 0.0 copy-done.1
  55.0 1.5 %band.1 = bf16[8,512,128]{2,1,0:T(8,128)(2,1)S(1)} custom-call(s32[8]{0:T(128)S(1)} %copy-done.1, f32[528,128]{1,0:T(8,128)S(1)} %bitcast.12, f32[528,128]{1,0:T(8,128)S(1)} %bitcast.11, f32[8,640]{1,0:T(8,128)S(1)} %slice_bitcast_fusion.side_ref, f32[8,512]{1,0:T(8,128)S(1)} %copy-done), custom_call_target="tpu_custom_call" | custom-call | tf_op jit(solution)/shard_map/band/pallas_call | solution.py:339
  56.5 20.0 %all_to_all.10 = bf16[8,512,128]{2,1,0:T(8,128)(2,1)S(1)} all-to-all(bf16[8,512,128]{2,1,0:T(8,128)(2,1)S(1)} %band.1), channel_id=1, replica_groups=mesh['zh'=2,'zl'=4,'yh'=2,'core'=2,'yl'=2,'x'=4] {'x','yl'}, dimensions={0} | all-to-all | bytes 2097152 | tf_op jit(solution)/shard_map/all_to_all | solution.py:382
  76.5 0.8 %convert_reduce_fusion = f32[512,128]{1,0:T(8,128)} fusion(bf16[8,512,128]{2,1,0:T(8,128)(2,1)S(1)} %all_to_all.10), kind=kLoop, calls=%fused_computation | loop fusion | flops 983040 | bytes 1310720 | tf_op jit(solution)/shard_map/reduce_sum | solution.py:383
  (2 shorter events, 0.0 us)
Async XLA Ops:
  1.8 21.4 %all-to-all-start = ((bf16[8,192,128]{2,1,0:T(8,128)(2,1)}), bf16[8,192,128]{2,1,0:T(8,128)(2,1)S(1)}, u32[]{:S(2)}, u32[]{:S(2)}) async-start(bf16[8,192,128]{2,1,0:T(8,128)(2,1)} %get-tuple-element.12), calls=%async_computation | async-start | bytes 786432 | tf_op jit(solution)/shard_map/all_to_all | solution.py:365
  10.4 8.3 %collective-permute-start = (bf16[8,512]{1,0:T(8,128)(2,1)}, bf16[8,512]{1,0:T(8,128)(2,1)S(1)}, u32[]{:S(2)}, u32[]{:S(2)}) collective-permute-start(bf16[8,512]{1,0:T(8,128)(2,1)} %get-tuple-element.11), channel_id=1, source_target_pairs={{8,16},{24,32},{40,48},{56,64},{72,80},{88,96},{104,112},{120,128}... | collective-permute-start | bytes 24584 | tf_op jit(solution)/shard_map/ppermute | solution.py:364
  18.7 7.7 %collective-permute-start.1 = (bf16[16,512]{1,0:T(8,128)(2,1)S(1)}, bf16[16,512]{1,0:T(8,128)(2,1)S(1)}, u32[]{:S(2)}, u32[]{:S(2)}) collective-permute-start(bf16[16,512]{1,0:T(8,128)(2,1)S(1)} %constant_dynamic-update-slice_fusion.refs_1_), channel_id=1, source_target_pairs={{0,8},{8,0},{1,9},{9,1},{2,10},{10,2},{3,11},{11,3},{4,12},{12,4},... | collective-permute-start | bytes 49160 | tf_op jit(solution)/shard_map/ppermute | solution.py:367
  23.3 16.8 %collective-permute-start.2 = (bf16[8,192,128]{2,1,0:T(8,128)(2,1)S(1)}, bf16[8,192,128]{2,1,0:T(8,128)(2,1)S(1)}, u32[]{:S(2)}, u32[]{:S(2)}) collective-permute-start(bf16[8,192,128]{2,1,0:T(8,128)(2,1)S(1)} %all-to-all-done.refs_3_), channel_id=1, source_target_pairs={{0,16},{16,0},{1,17},{17,1},{2,18},{18,2},{3,19},{19,3},{4,20},{20... | collective-permute-start | bytes 1179656 | tf_op jit(solution)/shard_map/ppermute | solution.py:372
  48.0 7.0 %collective-permute-start.3 = (f32[1,528,128]{2,1,0:T(8,128)S(1)}, f32[1,528,128]{2,1,0:T(8,128)S(1)}, u32[]{:S(2)}, u32[]{:S(2)}) collective-permute-start(f32[1,528,128]{2,1,0:T(8,128)S(1)} %get-tuple-element.16), channel_id=1, source_target_pairs={{0,8},{8,0},{1,9},{9,1},{2,10},{10,2},{3,11},{11,3},{4,12},{12,4},... | collective-permute-start | bytes 811016 | tf_op jit(solution)/shard_map/ppermute | solution.py:376
  48.1 6.9 %copy-start = (f32[8,512]{1,0:T(8,128)S(1)}, f32[8,512]{1,0:T(8,128)}, u32[]{:S(2)}) copy-start(f32[8,512]{1,0:T(8,128)} %band_ref.1) | copy-start | bytes 49156
  48.1 6.9 %copy-start.1 = (s32[8]{0:T(128)S(1)}, s32[8]{0:T(128)}, u32[]{:S(2)}) copy-start(s32[8]{0:T(128)} %offsets_ref.1) | copy-start | bytes 100
